TPU v7x, 128 devices: a whole 4x4x4 slice. The times are simulated.
128 devices in a mesh: rep: 32 (over y, z, core), shard: 4 (over x).
Axes of the slice: x: 4, y: 4, z: 4, core: 2. Of those that a mesh axis runs over, the one named last changes fastest.
Arguments:
- hidden: bfloat16 [128, 256, 768], P('rep', 'shard'), may hold values from -6 to 6
- grad_out: bfloat16 [128, 256, 768], P('rep', 'shard'), may hold values from -6 to 6
- lengths: int32 [128], P('rep'), may hold values from 1 to 256, 20480 in all
- bucket: int32 [511], replicated, may hold values from 1 to 511, as said below
- w_query: bfloat16 [768, 768], P('shard'), may hold values from -0.21875 to 0.21875
- w_key: bfloat16 [768, 768], P('shard'), may hold values from -0.21875 to 0.21875
- w_value: bfloat16 [768, 768], P('shard'), may hold values from -0.21875 to 0.21875
- w_out: bfloat16 [768, 768], P('shard'), may hold values from -1.25 to 1.25
- w_inner: bfloat16 [768, 3072], P('shard'), may hold values from -0.21875 to 0.21875
- w_outer: bfloat16 [3072, 768], P('shard'), may hold values from -0.109375 to 0.109375
- rel_table: bfloat16 [512, 768], P('shard'), may hold values from -6 to 6
- ln1_gain: bfloat16 [768], P('shard'), may hold values from 0.5 to 1.5
- ln1_bias: bfloat16 [768], P('shard'), may hold values from -1.5 to 1.5
- ln2_gain: bfloat16 [768], P('shard'), may hold values from 0.5 to 1.5
- ln2_bias: bfloat16 [768], P('shard'), may hold values from -1.5 to 1.5
Outputs:
- layer_output: bfloat16 [128, 256, 768], P('rep', 'shard')
- grad_hidden: bfloat16 [128, 256, 768], P('rep', 'shard')
- grad_w_query: float32 [768, 768], P('shard')
- grad_w_key: float32 [768, 768], P('shard')
- grad_w_value: float32 [768, 768], P('shard')
- grad_w_out: float32 [768, 768], P('shard')
- grad_w_inner: float32 [768, 3072], P('shard')
- grad_w_outer: float32 [3072, 768], P('shard')
- grad_rel_table: float32 [512, 768], P('shard')
- grad_ln1_gain: float32 [768], P('shard')
- grad_ln1_bias: float32 [768], P('shard')
- grad_ln2_gain: float32 [768], P('shard')
- grad_ln2_bias: float32 [768], P('shard')
- rms_values: float32 [4], replicated
Inputs may be any that keep to these rules, and one draw needn't show every extreme that they name: bucket[255 + d] = 256 + d for |d| < 128; beyond that it moves away from 256 monotonically with |d|, symmetric in the sign of d, several offsets sharing a row.
All inputs are finite; a program needn't handle non-finite values. No bound on the sum of `lengths` on one device may be relied on, other than what follows from the above.
Results may differ from a plain program's by a relative error of at most 0.028.
Values may be sent and summed in bfloat16 or wider, within the bound.
No kernel may reach another device: no remote copies, remote signals or barrier semaphores. Data moves between devices by JAX's collectives and lax.ppermute only.
A program may use at most 192 MiB of HBM per device.

v0:
```python
import jax
import jax.numpy as jnp
from jax import lax
from jax.sharding import PartitionSpec as P

D = 768
HEADS = 12
HEAD_DIM = 64


EPSILON = 1e-07
MASKED = -1e30


def side_by_side(arrays, axis, split_dim, concat_dim, along):
    ends, at = ([], 0)
    for a in arrays[:-1]:
        at += a.shape[along]
        ends.append(at)
    both = jnp.concatenate(arrays, axis=along)
    return tuple(
        jnp.split(
            lax.all_to_all(both, axis, split_axis=split_dim, concat_axis=concat_dim, tiled=True),
            ends,
            axis=along,
        )
    )


def sent_together(arrays, axis, dim, along):
    ends, at = ([], 0)
    for a in arrays[:-1]:
        at += a.shape[along]
        ends.append(at)
    both = jnp.concatenate(arrays, axis=along)
    return tuple(jnp.split(lax.all_gather(both, axis, axis=dim, tiled=True), ends, axis=along))


def heads_split(matrix):
    number = matrix.shape[0]
    return matrix.reshape(number, HEADS, HEAD_DIM).transpose(1, 0, 2)


def heads_join(stacked):
    return stacked.transpose(1, 0, 2).reshape(stacked.shape[1], HEADS * HEAD_DIM)


def norm_forward(values, gain, shift):
    center = values - jnp.mean(values, axis=1, keepdims=True)
    inverse = lax.rsqrt(jnp.mean(center * center, axis=1, keepdims=True) + EPSILON)
    normed = center * inverse
    return (normed * gain + shift, normed, inverse)


def norm_backward(upstream, normed, inverse, gain):
    scaled = upstream * gain
    plain_mean = jnp.mean(scaled, axis=1, keepdims=True)
    cross_mean = jnp.mean(scaled * normed, axis=1, keepdims=True)
    return inverse * (scaled - plain_mean - normed * cross_mean)


def skew_rows(offset_rows):
    count = offset_rows.shape[0]
    flat = jnp.concatenate(
        [offset_rows[:, ::-1], jnp.zeros((count, 1), offset_rows.dtype)], axis=1
    ).reshape(-1)
    window = lax.slice_in_dim(flat, count - 1, count - 1 + count * (2 * count - 1))
    return window.reshape(count, 2 * count - 1)[:, :count]


def unskew_rows(square):
    count = square.shape[0]
    widened = jnp.concatenate(
        [square, jnp.zeros((count, count - 1), square.dtype)], axis=1
    ).reshape(-1)
    placed = jnp.concatenate(
        [jnp.zeros((count - 1,), square.dtype), widened, jnp.zeros((1,), square.dtype)]
    ).reshape(count, 2 * count)
    return placed[:, : 2 * count - 1][:, ::-1]


def head_scores(query_head, key_head, posk_wide, posq_wide, key_valid):
    scaling = (3.0 * HEAD_DIM) ** (-0.5)
    content = jnp.einsum("le,me->lm", query_head, key_head, preferred_element_type=jnp.float32)
    to_offsets = jnp.einsum("le,oe->lo", query_head, posk_wide, preferred_element_type=jnp.float32)
    from_offsets = jnp.einsum("me,oe->mo", key_head, posq_wide, preferred_element_type=jnp.float32)
    to_gather = skew_rows(to_offsets)
    from_gather = skew_rows(from_offsets).T
    return jnp.where(key_valid[None, :], (content + to_gather + from_gather) * scaling, MASKED)


def shards(
    hidden,
    grad_out,
    lengths,
    bucket,
    w_query,
    w_key,
    w_value,
    w_out,
    w_inner,
    w_outer,
    rel_table,
    ln1_gain,
    ln1_bias,
    ln2_gain,
    ln2_bias,
):
    members = lax.axis_size("shard")
    member = lax.axis_index("shard")
    slot_ids = jnp.arange(members, dtype=jnp.int32)
    longer = (lengths[None, :] > lengths[:, None]) | (lengths[None, :] == lengths[:, None]) & (
        slot_ids[None, :] < slot_ids[:, None]
    )
    dealing = jnp.sum(longer.astype(jnp.int32), axis=1)
    chosen = (dealing[None, :] == slot_ids[:, None]).astype(jnp.int32)
    source_of = jnp.sum(chosen * slot_ids[None, :], axis=1)
    arrived, arrived_grad = side_by_side(
        (jnp.take(hidden, source_of, axis=0), jnp.take(grad_out, source_of, axis=0)),
        "shard",
        0,
        1,
        2,
    )
    tokens = arrived[0]
    upstream = arrived_grad[0].astype(jnp.float32)
    length_here = jnp.sum(jnp.where(dealing == member, lengths, 0))
    row_count = tokens.shape[0]
    positions = jnp.arange(row_count, dtype=jnp.int32)
    key_valid = positions < length_here
    row_mask = key_valid.astype(jnp.float32)[:, None]
    scaling = (3.0 * HEAD_DIM) ** (-0.5)
    gathered = (
        *sent_together((w_query, w_key, w_value, w_out, w_inner), "shard", 0, 1),
        lax.all_gather(w_outer, "shard", axis=0, tiled=True),
        lax.all_gather(rel_table, "shard", axis=0, tiled=True),
        lax.all_gather(ln1_gain, "shard", axis=0, tiled=True),
        lax.all_gather(ln1_bias, "shard", axis=0, tiled=True),
        lax.all_gather(ln2_gain, "shard", axis=0, tiled=True),
        lax.all_gather(ln2_bias, "shard", axis=0, tiled=True),
    )
    (
        full_query,
        full_key,
        full_value,
        full_out,
        full_inner,
        full_outer,
        full_rel,
        gain_one,
        bias_one,
        gain_two,
        bias_two,
    ) = gathered
    table_rows = full_rel.shape[0]
    bucket_onehot = (bucket[:, None] == jnp.arange(table_rows, dtype=jnp.int32)[None, :]).astype(
        jnp.bfloat16
    )
    pos_key = jnp.dot(full_rel, full_key, preferred_element_type=jnp.float32).astype(jnp.bfloat16)
    pos_query = jnp.dot(full_rel, full_query, preferred_element_type=jnp.float32).astype(
        jnp.bfloat16
    )
    posk_wide = heads_split(jnp.take(pos_key, bucket, axis=0))
    posq_wide = heads_split(jnp.take(pos_query, bucket, axis=0))
    queries = jnp.dot(tokens, full_query, preferred_element_type=jnp.float32).astype(jnp.bfloat16)
    keys_all = jnp.dot(tokens, full_key, preferred_element_type=jnp.float32).astype(jnp.bfloat16)
    values_all = jnp.dot(tokens, full_value, preferred_element_type=jnp.float32).astype(
        jnp.bfloat16
    )
    head_inputs = (
        heads_split(queries),
        heads_split(keys_all),
        heads_split(values_all),
        posk_wide,
        posq_wide,
    )

    def head_forward(pieces):
        query_head, key_head, value_head, posk_head, posq_head = pieces
        scores = head_scores(query_head, key_head, posk_head, posq_head, key_valid)
        row_top = jnp.max(scores, axis=1, keepdims=True)
        shifted = jnp.exp(scores - row_top)
        summed = jnp.sum(shifted, axis=1, keepdims=True)
        probs_low = (shifted / summed).astype(jnp.bfloat16)
        context_head = jnp.einsum(
            "lm,me->le", probs_low, value_head, preferred_element_type=jnp.float32
        ).astype(jnp.bfloat16)
        return (context_head, (row_top + jnp.log(summed))[:, 0])

    contexts, lse_rows = lax.map(head_forward, head_inputs)
    context = heads_join(contexts)
    attn_out = jnp.dot(context, full_out, preferred_element_type=jnp.float32)
    token_float = tokens.astype(jnp.float32)
    gain_first = gain_one.astype(jnp.float32)
    gain_second = gain_two.astype(jnp.float32)
    hidden_one, normed_one, inverse_one = norm_forward(
        token_float + attn_out, gain_first, bias_one.astype(jnp.float32)
    )
    hidden_low = hidden_one.astype(jnp.bfloat16)
    inner_pre = jnp.dot(hidden_low, full_inner, preferred_element_type=jnp.float32)
    act_low = jax.nn.gelu(inner_pre, approximate=False).astype(jnp.bfloat16)
    ffn_out = jnp.dot(act_low, full_outer, preferred_element_type=jnp.float32)
    layer_full, normed_two, inverse_two = norm_forward(
        hidden_one + ffn_out, gain_second, bias_two.astype(jnp.float32)
    )
    layer_full = layer_full * row_mask
    squares = jnp.stack(
        [
            jnp.sum(token_float * token_float * row_mask),
            jnp.sum(attn_out * attn_out * row_mask),
            jnp.sum(ffn_out * ffn_out * row_mask),
            jnp.sum(layer_full * layer_full),
            length_here.astype(jnp.float32),
        ]
    )
    back_query, back_key, back_value, back_out, back_inner, back_outer, back_rel = gathered[:7]
    grad_y = upstream * row_mask
    grad_gain_two = jnp.sum(grad_y * normed_two, axis=0)
    grad_bias_two = jnp.sum(grad_y, axis=0)
    grad_resid_two = norm_backward(grad_y, normed_two, inverse_two, gain_second)
    grad_ffn = grad_resid_two.astype(jnp.bfloat16)
    grad_w_outer = jnp.einsum("lf,ld->fd", act_low, grad_ffn, preferred_element_type=jnp.float32)
    grad_act = jnp.einsum("ld,fd->lf", grad_ffn, back_outer, preferred_element_type=jnp.float32)
    cumulative = 0.5 * (1.0 + jax.scipy.special.erf(inner_pre * 0.5**0.5))
    density = jnp.exp(-0.5 * inner_pre * inner_pre) * (2.0 * jnp.pi) ** (-0.5)
    grad_inner = (grad_act * (cumulative + inner_pre * density)).astype(jnp.bfloat16)
    grad_w_inner = jnp.einsum(
        "ld,lf->df", hidden_low, grad_inner, preferred_element_type=jnp.float32
    )
    grad_hidden_one = grad_resid_two + jnp.einsum(
        "lf,df->ld", grad_inner, back_inner, preferred_element_type=jnp.float32
    )
    grad_gain_one = jnp.sum(grad_hidden_one * normed_one, axis=0)
    grad_bias_one = jnp.sum(grad_hidden_one, axis=0)
    grad_resid_one = norm_backward(grad_hidden_one, normed_one, inverse_one, gain_first)
    grad_attn = grad_resid_one.astype(jnp.bfloat16)
    grad_w_out = jnp.einsum("le,ld->ed", context, grad_attn, preferred_element_type=jnp.float32)
    grad_context = jnp.einsum(
        "ld,ed->le", grad_attn, back_out, preferred_element_type=jnp.float32
    ).astype(jnp.bfloat16)

    def head_back(pieces):
        (
            query_head,
            key_head,
            value_head,
            grad_head,
            lse_head,
            poskw_head,
            posqw_head,
            posk_head,
            posq_head,
        ) = pieces
        scores = head_scores(query_head, key_head, poskw_head, posqw_head, key_valid)
        probs = jnp.exp(scores - lse_head[:, None])
        grad_probs = jnp.einsum(
            "le,me->lm", grad_head, value_head, preferred_element_type=jnp.float32
        )
        grad_scores = (
            probs * (grad_probs - jnp.sum(probs * grad_probs, axis=1, keepdims=True))
        ).astype(jnp.bfloat16)
        grad_value = jnp.einsum(
            "lm,le->me", probs.astype(jnp.bfloat16), grad_head, preferred_element_type=jnp.float32
        ).astype(jnp.bfloat16)
        to_offsets = unskew_rows(grad_scores)
        from_offsets = unskew_rows(grad_scores.T)
        grad_to = (
            jnp.dot(to_offsets, bucket_onehot, preferred_element_type=jnp.float32) * scaling
        ).astype(jnp.bfloat16)
        grad_from = (
            jnp.dot(from_offsets, bucket_onehot, preferred_element_type=jnp.float32) * scaling
        ).astype(jnp.bfloat16)
        grad_query = (
            jnp.einsum("lm,me->le", grad_scores, key_head, preferred_element_type=jnp.float32)
            * scaling
            + jnp.einsum("lr,re->le", grad_to, posk_head, preferred_element_type=jnp.float32)
        ).astype(jnp.bfloat16)
        grad_key = (
            jnp.einsum("lm,le->me", grad_scores, query_head, preferred_element_type=jnp.float32)
            * scaling
            + jnp.einsum("mr,re->me", grad_from, posq_head, preferred_element_type=jnp.float32)
        ).astype(jnp.bfloat16)
        grad_posk = jnp.einsum("lr,le->re", grad_to, query_head, preferred_element_type=jnp.float32)
        grad_posq = jnp.einsum("mr,me->re", grad_from, key_head, preferred_element_type=jnp.float32)
        return (grad_query, grad_key, grad_value, grad_posk, grad_posq)

    head_grads = lax.map(
        head_back,
        (
            head_inputs[0],
            head_inputs[1],
            head_inputs[2],
            heads_split(grad_context),
            lse_rows,
            posk_wide,
            posq_wide,
            heads_split(pos_key),
            heads_split(pos_query),
        ),
    )
    grad_queries = heads_join(head_grads[0])
    grad_keys = heads_join(head_grads[1])
    grad_values = heads_join(head_grads[2])
    grad_tokens = grad_resid_one + jnp.einsum(
        "le,de->ld", grad_queries, back_query, preferred_element_type=jnp.float32
    )
    grad_tokens = grad_tokens + jnp.einsum(
        "le,de->ld", grad_keys, back_key, preferred_element_type=jnp.float32
    )
    grad_tokens = grad_tokens + jnp.einsum(
        "le,de->ld", grad_values, back_value, preferred_element_type=jnp.float32
    )
    grad_w_query = jnp.einsum("ld,le->de", tokens, grad_queries, preferred_element_type=jnp.float32)
    grad_w_key = jnp.einsum("ld,le->de", tokens, grad_keys, preferred_element_type=jnp.float32)
    grad_w_value = jnp.einsum("ld,le->de", tokens, grad_values, preferred_element_type=jnp.float32)
    posk_total, posq_total, stat_totals = lax.psum(
        (heads_join(head_grads[3]), heads_join(head_grads[4]), squares), ("rep", "shard")
    )
    posk_low = posk_total.astype(jnp.bfloat16)
    posq_low = posq_total.astype(jnp.bfloat16)
    rel_rows = rel_table.shape[0]
    model_rows = w_query.shape[0]
    posk_mine = lax.dynamic_slice_in_dim(posk_low, member * rel_rows, rel_rows, 0)
    posq_mine = lax.dynamic_slice_in_dim(posq_low, member * rel_rows, rel_rows, 0)
    grad_rel = jnp.einsum(
        "re,de->rd", posk_mine, back_key, preferred_element_type=jnp.float32
    ) + jnp.einsum("re,de->rd", posq_mine, back_query, preferred_element_type=jnp.float32)
    rel_columns = lax.dynamic_slice_in_dim(back_rel, member * model_rows, model_rows, 1)
    key_extra = jnp.einsum("rd,re->de", rel_columns, posk_low, preferred_element_type=jnp.float32)
    query_extra = jnp.einsum("rd,re->de", rel_columns, posq_low, preferred_element_type=jnp.float32)
    (
        share_q,
        share_k,
        share_v,
        share_o,
        share_in,
        share_outer,
        share_g1,
        share_b1,
        share_g2,
        share_b2,
    ) = (
        lax.psum_scatter(
            grad_w_query.astype(jnp.bfloat16), "shard", scatter_dimension=0, tiled=True
        ).astype(jnp.float32),
        lax.psum_scatter(
            grad_w_key.astype(jnp.bfloat16), "shard", scatter_dimension=0, tiled=True
        ).astype(jnp.float32),
        lax.psum_scatter(
            grad_w_value.astype(jnp.bfloat16), "shard", scatter_dimension=0, tiled=True
        ).astype(jnp.float32),
        lax.psum_scatter(
            grad_w_out.astype(jnp.bfloat16), "shard", scatter_dimension=0, tiled=True
        ).astype(jnp.float32),
        lax.psum_scatter(
            grad_w_inner.astype(jnp.bfloat16), "shard", scatter_dimension=0, tiled=True
        ).astype(jnp.float32),
        lax.psum_scatter(
            grad_w_outer.astype(jnp.bfloat16), "shard", scatter_dimension=0, tiled=True
        ).astype(jnp.float32),
        lax.psum_scatter(
            grad_gain_one.astype(jnp.bfloat16), "shard", scatter_dimension=0, tiled=True
        ).astype(jnp.float32),
        lax.psum_scatter(
            grad_bias_one.astype(jnp.bfloat16), "shard", scatter_dimension=0, tiled=True
        ).astype(jnp.float32),
        lax.psum_scatter(
            grad_gain_two.astype(jnp.bfloat16), "shard", scatter_dimension=0, tiled=True
        ).astype(jnp.float32),
        lax.psum_scatter(
            grad_bias_two.astype(jnp.bfloat16), "shard", scatter_dimension=0, tiled=True
        ).astype(jnp.float32),
    )
    (
        total_q,
        total_k,
        total_v,
        total_o,
        total_in,
        total_outer,
        total_g1,
        total_b1,
        total_g2,
        total_b2,
    ) = (
        lax.psum(share_q.astype(jnp.bfloat16), "rep").astype(jnp.float32),
        lax.psum(share_k.astype(jnp.bfloat16), "rep").astype(jnp.float32),
        lax.psum(share_v.astype(jnp.bfloat16), "rep").astype(jnp.float32),
        lax.psum(share_o.astype(jnp.bfloat16), "rep").astype(jnp.float32),
        lax.psum(share_in.astype(jnp.bfloat16), "rep").astype(jnp.float32),
        lax.psum(share_outer.astype(jnp.bfloat16), "rep").astype(jnp.float32),
        lax.psum(share_g1.astype(jnp.bfloat16), "rep").astype(jnp.float32),
        lax.psum(share_b1.astype(jnp.bfloat16), "rep").astype(jnp.float32),
        lax.psum(share_g2.astype(jnp.bfloat16), "rep").astype(jnp.float32),
        lax.psum(share_b2.astype(jnp.bfloat16), "rep").astype(jnp.float32),
    )
    rms_values = jnp.sqrt(stat_totals[:4] / (stat_totals[4] * D))
    returned, returned_grad = side_by_side(
        (layer_full.astype(jnp.bfloat16)[None], grad_tokens.astype(jnp.bfloat16)[None]),
        "shard",
        1,
        0,
        2,
    )
    layer_output = jnp.take(returned, dealing, axis=0)
    grad_hidden = jnp.take(returned_grad, dealing, axis=0)
    return (
        layer_output,
        grad_hidden,
        total_q + query_extra,
        total_k + key_extra,
        total_v,
        total_o,
        total_in,
        total_outer,
        grad_rel,
        total_g1,
        total_b1,
        total_g2,
        total_b2,
        rms_values,
    )


def solution(mesh):
    return jax.shard_map(
        shards,
        mesh=mesh,
        in_specs=(
            P("rep", "shard", None),
            P("rep", "shard", None),
            P("rep"),
            P(),
            P("shard", None),
            P("shard", None),
            P("shard", None),
            P("shard", None),
            P("shard", None),
            P("shard", None),
            P("shard", None),
            P("shard"),
            P("shard"),
            P("shard"),
            P("shard"),
        ),
        out_specs=(
            P("rep", "shard", None),
            P("rep", "shard", None),
            P("shard", None),
            P("shard", None),
            P("shard", None),
            P("shard", None),
            P("shard", None),
            P("shard", None),
            P("shard", None),
            P("shard"),
            P("shard"),
            P("shard"),
            P("shard"),
            P(),
        ),
        check_vma=False,
    )
```

profile of v0, /device:TPU:17, one launch (start us, length us, event | category | flops | bytes accessed | tf_op | source)
XLA Modules:
  0.0 953.8 jit_solution(6435139361487600487)
XLA Ops:
  18.6 4.0 all-to-all-start
  26.9 9.9 %all-reduce.18 = (bf16[768]{0:T(1024)(128)(2,1)S(1)}, bf16[768]{0:T(1024)(128)(2,1)S(1)}, bf16[768]{0:T(1024)(128)(2,1)S(1)}, bf16[768]{0:T(1024)(128)(2,1)S(1)}) all-reduce(bf16[768]{0:T(1024)(128)(2,1)S(1)} %dynamic-update-slice.1, bf16[768]{0:T(1024)(128)(2,1)S(1)} %dynamic-update-slice, ...), channel_id=1, replica_groups=mesh['rep'=32,'shard'=4] {'shard'}, use_global_device_ids=true, to_apply=%add.7 | all-reduce | flops 3072 | bytes 12288
  38.6 15.9 %all_gather.22 = bf16[512,768]{1,0:T(8,128)(2,1)S(1)} all-gather(bf16[128,768]{1,0:T(8,128)(2,1)S(1)} %copy-done.27), channel_id=1, replica_groups=mesh['rep'=32,'shard'=4] {'shard'}, dimensions={0}, use_global_device_ids=true | all-gather | bytes 983040 | tf_op jit(solution)/shard_map/all_gather | solution.py:136
  54.5 63.7 %all-gather.3.cloned.1.call-done = bf16[768,6144]{1,0:T(8,128)(2,1)} async-done(((bf16[192,6144]{1,0:T(8,128)(2,1)}), bf16[768,6144]{1,0:T(8,128)(2,1)}) %all-gather.3.cloned.1.call-update) | async-done | bytes 9437200 | tf_op jit(solution)/shard_map/all_gather | solution.py:36
  132.9 2.9 gather_fusion.2
  135.8 2.7 gather_fusion.3
  143.5 123.1 %while.32 = (s32[]{:T(128)}, bf16[12,256,64]{1,2,0:T(8,128)(2,1)S(1)}, f32[12,256]{1,0:T(8,128)}, bf16[12,256,64]{2,1,0:T(8,128)(2,1)}, bf16[12,256,64]{2,1,0:T(...) while((s32[]{:T(128)}, ...), condition=%wide.region_6.9_spmd.clone, body=%wide.region_3.8_spmd.clone.sunk | while | flops 50937856 | bytes 16611957 | solution.py:190
  266.6 2.7 fusion.180
  270.1 10.9 %fusion.112 = (bf16[256,3072]{1,0:T(8,128)(2,1)S(1)}, f32[256,3072]{1,0:T(8,128)}) fusion(bf16[768,6144]{1,0:T(8,128)(2,1)} %all-gather.3.cloned.1.call-done, f32[256,768]{1,0:T(8,128)S(1)} %get-tuple-element.418, f32[768]{0:T(1024)S(1)} %convert_element_type.206, f32[768]{0:T(1024)S(1)} %convert_element_type.205, f32[256]{0:T(256)S(1)} %add_rsqrt_fusion.1, ...), kind=kOutput, calls=%fused_computation.143 | convolution fusion | flops 1260060672 | bytes 10231808 | tf_op jit(solution)/shard_map/dot_general | solution.py:200
  281.0 4.4 fusion.178
  287.9 3.6 fusion.109
  304.2 323.5 %while.33 = (s32[]{:T(128)}, bf16[12,256,64]{1,2,0:T(8,128)(2,1)S(1)}, bf16[12,256,64]{1,2,0:T(8,128)(2,1)}, bf16[12,256,64]{1,2,0:T(8,128)(2,1)}, f32[12,512,64...) while((s32[]{:T(128)}, ...), condition=%wide.region_17.20_spmd.clone, body=%wide.region_15.19_spmd.clone.sunk | while | flops 412858368 | bytes 26322116 | solution.py:287
  633.6 5.4 convolution_convert_fusion.2
  639.7 5.1 convolution_convert_fusion.3
  646.2 2.6 stack.23
  648.8 111.7 %all-reduce.23 = (bf16[512,768]{0,1:T(8,128)(2,1)}, bf16[512,768]{0,1:T(8,128)(2,1)}, f32[5]{0:T(128)S(1)}) all-reduce(f32[512,768]{0,1:T(8,128)} %bitcast.393, f32[512,768]{0,1:T(8,128)} %bitcast.392, f32[5]{0:T(128)S(1)} %stack.23), channel_id=1, replica_groups=mesh['rep'=32,'shard'=4] {'rep','shard'}, use_global_device_ids=true, to_apply=%region_20.23 | all-reduce | flops 786437 | bytes 4718632 | tf_op jit(solution)/shard_map/psum | solution.py:316
  764.9 4.5 reduce-scatter.17.cloned.1.call-done
  769.4 53.0 %reduce-scatter.15.cloned.1.call-done = bf16[192,3072]{1,0:T(8,128)(2,1)} async-done(((bf16[768,3072]{1,0:T(8,128)(2,1)}), bf16[192,3072]{1,0:T(8,128)(2,1)}) %reduce-scatter.15.cloned.1.call-update) | async-done | bytes 1179664 | tf_op jit(solution)/shard_map/reduce_scatter | solution.py:355
  826.1 5.5 reduce
  833.0 3.5 all-to-all-start.1
  837.7 12.2 %all-reduce.17 = (bf16[768]{0:T(1024)(128)(2,1)S(1)}, bf16[768]{0:T(1024)(128)(2,1)S(1)}, bf16[768]{0:T(1024)(128)(2,1)S(1)}, bf16[768]{0:T(1024)(128)(2,1)S(1)}) all-reduce(bf16[768]{0:T(1024)(128)(2,1)S(1)} %copy-done.49, bf16[768]{0:T(1024)(128)(2,1)S(1)} %copy-done.50, ...), channel_id=8, replica_groups=mesh['rep'=32,'shard'=4] {'shard'}, use_global_device_ids=true, to_apply=%region_33.36.clone | all-reduce | flops 3072 | bytes 12288
  850.2 55.0 %all-reduce.15 = (bf16[192]{0:T(256)(128)(2,1)S(1)}, bf16[192]{0:T(256)(128)(2,1)S(1)}, bf16[192]{0:T(256)(128)(2,1)S(1)}, bf16[192]{0:T(256)(128)(2,1)S(1)}) all-reduce(bf16[192]{0:T(256)(128)(2,1)S(1)} %dynamic-slice.5, bf16[192]{0:T(256)(128)(2,1)S(1)} %dynamic-slice.7, ...), channel_id=1, replica_groups=mesh['rep'=32,'shard'=4] {'rep'}, use_global_device_ids=true, to_apply=%region_34.37 | all-reduce | flops 768 | bytes 3072 | tf_op jit(solution)/shard_map/psum | solution.py:392
  915.2 22.6 %all-reduce.22.cloned.1.call-done = (bf16[192,768]{1,0:T(8,128)(2,1)}, bf16[192,768]{1,0:T(8,128)(2,1)}, bf16[192,768]{1,0:T(8,128)(2,1)}, bf16[192,768]{1,0:T(8...) async-done(((bf16[192,768]{1,0:T(8,128)(2,1)}, bf16[192,768]{1,0:T(8,128)(2,1)}, bf16[192,768]{1,0:T(8,128)(2,1)}, bf16[192,768]{1,0:T(8,128)(2,1)}, ...) | async-done | bytes 3538960 | tf_op jit(solution)/shard_map/psum | solution.py:386
  937.8 3.1 convert_element_type.232
  (1049 shorter events, 526.6 us)
Async XLA Ops:
  7.2 111.0 %all-gather.3.cloned.1.call-start = ((), (), s32[]{:S(2)}) async-start(), calls=%async_computation.8 | async-start | bytes 11796480 | tf_op jit(solution)/shard_map/all_gather | solution.py:36
  16.9 9.0 copy-start.52
  16.9 9.3 copy-start.53
  16.9 9.5 copy-start.54
  16.9 9.7 %copy-start.55 = (bf16[192]{0:T(256)(128)(2,1)S(1)}, bf16[192]{0:T(256)(128)(2,1)}, u32[]{:S(2)}) copy-start(bf16[192]{0:T(256)(128)(2,1)} %param.37) | copy-start | bytes 1156
  16.9 21.7 %copy-start.27 = (bf16[128,768]{1,0:T(8,128)(2,1)S(1)}, bf16[128,768]{1,0:T(8,128)(2,1)}, u32[]{:S(2)}) copy-start(bf16[128,768]{1,0:T(8,128)(2,1)} %param.33) | copy-start | bytes 589828
  18.6 35.9 %all-to-all-start = ((bf16[4,64,1536]{2,1,0:T(8,128)(2,1)}), bf16[4,64,1536]{2,1,0:T(8,128)(2,1)S(1)}, u32[]{:S(2)}, u32[]{:S(2)}) async-start(bf16[4,64,1536]{2,1,0:T(8,128)(2,1)} %pad_maximum_fusion), calls=%async_computation | async-start | bytes 1572864 | tf_op jit(solution)/shard_map/all_to_all | solution.py:23
  22.6 258.3 %all-gather.5.cloned.1.call-start = ((), (), s32[]{:S(2)}) async-start(), calls=%async_computation.9 | async-start | bytes 5898240 | tf_op jit(solution)/shard_map/all_gather | solution.py:135
  23.4 741.5 %reduce-scatter.13.cloned.1.call-start = ((), (), s32[]{:S(2)}) async-start(), calls=%async_computation.13 | async-start | bytes 1474560 | tf_op jit(solution)/shard_map/reduce_scatter | solution.py:352
  54.5 73.1 %copy-start.14 = (bf16[512,768]{1,0:T(8,128)(2,1)}, bf16[512,768]{1,0:T(8,128)(2,1)S(1)}, u32[]{:S(2)}) copy-start(bf16[512,768]{1,0:T(8,128)(2,1)S(1)} %all_gather.22) | copy-start | bytes 2359300
  302.5 462.4 %reduce-scatter.11.cloned.1.call-start = ((), (), s32[]{:S(2)}) async-start(), calls=%async_computation.12 | async-start | bytes 1474560 | tf_op jit(solution)/shard_map/reduce_scatter | solution.py:349
  630.2 134.7 %reduce-scatter.7.cloned.1.call-start = ((), (), s32[]{:S(2)}) async-start(), calls=%async_computation.10 | async-start | bytes 1474560 | tf_op jit(solution)/shard_map/reduce_scatter | solution.py:343
  631.9 133.0 %reduce-scatter.9.cloned.1.call-start = ((), (), s32[]{:S(2)}) async-start(), calls=%async_computation.11 | async-start | bytes 1474560 | tf_op jit(solution)/shard_map/reduce_scatter | solution.py:346
  633.5 135.9 %reduce-scatter.17.cloned.1.call-start = ((), (), s32[]{:S(2)}) async-start(), calls=%async_computation.15 | async-start | bytes 5898240 | tf_op jit(solution)/shard_map/reduce_scatter | solution.py:358
  639.0 183.4 %reduce-scatter.15.cloned.1.call-start = ((), (), s32[]{:S(2)}) async-start(), calls=%async_computation.14 | async-start | bytes 5898240 | tf_op jit(solution)/shard_map/reduce_scatter | solution.py:355
  644.8 116.3 %copy-start.3 = (f32[256,768]{1,0:T(8,128)S(1)}, f32[256,768]{1,0:T(8,128)}, u32[]{:S(2)}) copy-start(f32[256,768]{1,0:T(8,128)} %copy-done.2) | copy-start | bytes 2359300
  644.9 292.9 %all-reduce.22.cloned.1.call-start = ((), (), s32[]{:S(2)}) async-start(), calls=%async_computation.16 | async-start | bytes 7077888 | tf_op jit(solution)/shard_map/psum | solution.py:386
  763.0 59.5 %copy-start.8 = (bf16[12,256,64]{1,2,0:T(8,128)(2,1)S(1)}, bf16[12,256,64]{1,2,0:T(8,128)(2,1)}, u32[]{:S(2)}) copy-start(bf16[12,256,64]{1,2,0:T(8,128)(2,1)} %get-tuple-element.159) | copy-start | bytes 1179652
  825.6 12.1 %copy-start.36 = (bf16[768]{0:T(1024)(128)(2,1)S(1)}, bf16[768]{0:T(1024)(128)(2,1)}, u32[]{:S(2)}) copy-start(bf16[768]{0:T(1024)(128)(2,1)} %get-tuple-element.334) | copy-start | bytes 4612
  825.6 12.1 %copy-start.37 = (bf16[768]{0:T(1024)(128)(2,1)S(1)}, bf16[768]{0:T(1024)(128)(2,1)}, u32[]{:S(2)}) copy-start(bf16[768]{0:T(1024)(128)(2,1)} %get-tuple-element.338) | copy-start | bytes 4612
  825.6 12.1 %copy-start.49 = (bf16[768]{0:T(1024)(128)(2,1)S(1)}, bf16[768]{0:T(1024)(128)(2,1)}, u32[]{:S(2)}) copy-start(bf16[768]{0:T(1024)(128)(2,1)} %get-tuple-element.328) | copy-start | bytes 4612
  825.6 12.1 %copy-start.50 = (bf16[768]{0:T(1024)(128)(2,1)S(1)}, bf16[768]{0:T(1024)(128)(2,1)}, u32[]{:S(2)}) copy-start(bf16[768]{0:T(1024)(128)(2,1)} %get-tuple-element.339) | copy-start | bytes 4612
  826.1 83.3 %copy-start.18 = (bf16[512,768]{0,1:T(8,128)(2,1)S(1)}, bf16[512,768]{0,1:T(8,128)(2,1)}, u32[]{:S(2)}) copy-start(bf16[512,768]{0,1:T(8,128)(2,1)} %get-tuple-element.394) | copy-start | bytes 2359300
  833.0 79.0 %all-to-all-start.1 = ((bf16[4,2,49152]{2,1,0:T(2,128)(2,1)}), bf16[4,2,49152]{2,1,0:T(2,128)(2,1)S(1)}, u32[]{:S(2)}, u32[]{:S(2)}) async-start(bf16[4,2,49152]{2,1,0:T(2,128)(2,1)} %reshape.324), calls=%async_computation.1 | async-start | bytes 1572864 | tf_op jit(solution)/shard_map/all_to_all | solution.py:23
  (60 other events, 284.2 us)
Sparse Core Ops, SparseCore 0:
  15.5 102.7 all-gather.2
  119.9 52.6 all-gather.4
  302.6 22.9 reduce-scatter.12
  630.4 22.8 reduce-scatter.10
  656.1 25.6 reduce-scatter.6
  684.6 23.2 reduce-scatter.8
  710.2 59.1 reduce-scatter.16
  771.8 50.5 reduce-scatter.14
  826.6 111.0 all-reduce.21
where the time goes:
time: 969 us; the launch traced here: 954 us
  matrix products  302 us (31%)
  local copies, waits for them, and re-layouts  231 us (24%)
  blocking collectives  205 us (21%)
  waiting for transfers between devices  145 us (15%)
  other arithmetic  41.7 us (4%)
  between operations  17.7 us (2%)
    psum x1, blocking collectives, shards(): lax.psum((heads_join(head_grads[3]), heads_join(head_grads[4]), squares),...  112 us
    while x276, local copies, waits for them, and re-layouts  79.3 us
    all_gather x1, waiting for transfers between devices, sent_together(): lax.all_gather(both, axis, axis=dim, tiled=True)  63.7 us
    psum x1, blocking collectives, shards(): lax.psum(share_g1.astype(jnp.bfloat16), 'rep').astype(jnp.float32)  55 us
    reduce_scatter x1, waiting for transfers between devices, shards(): lax.psum_scatter(grad_w_inner.astype(jnp.bfloat16), 'shard', scatter_dime...  53 us
    concatenate x24, local copies, waits for them, and re-layouts, unskew_rows(): jnp.concatenate([jnp.zeros((count - 1,), square.dtype), widened, jnp.zero...  37.8 us
    dot_general x24, matrix products, head_scores(): jnp.einsum('me,oe->mo', key_head, posq_wide, preferred_element_type=jnp.f...  28.2 us
    dot_general x24, matrix products, head_scores(): jnp.einsum('le,oe->lo', query_head, posk_wide, preferred_element_type=jnp...  28.1 us
  transfers between devices with their start and end apart: 11, of which 4 were waited for; matrix products, arithmetic and copies ran while one was open for 56% of the time, Pallas kernels for 0%

commit v1 on v0

v1 whole, which is shorter than its diff:
```python
import jax
import jax.numpy as jnp
from jax import lax
from jax.experimental import pallas as pl
from jax.experimental.pallas import tpu as pltpu
from jax.sharding import Mesh
from jax.sharding import PartitionSpec as P

D = 768
HEADS = 12
HEAD_DIM = 64
PAIRS = HEADS // 2
ROWS = 256
OFFS = 512
TOKENS = 20480
GROUP = 4
PIECE = D // GROUP
HALF = PIECE // 2
WIDE = GROUP * D
REL_HALF = OFFS // GROUP // 2
REL_AT = 3 * HALF
FIRST = 3 * HALF + REL_HALF
OUT_AT = D // 2
NORM_AT = D // 2 + HALF
SECOND = D // 2 + HALF + 16
META_LENGTH, META_CORE, META_SLOT, META_KEEP, META_SEND = 0, 1, 2, 6, 10
EPSILON = 1e-07
MASKED = -1e30
SCALING = (3.0 * HEAD_DIM) ** (-0.5)
F32 = jnp.float32
LOW = jnp.bfloat16
MIB = 1024 * 1024


def mm(a, b):
    return lax.dot_general(a, b, (((1,), (0,)), ((), ())), preferred_element_type=F32)


def mm_nt(a, b):
    return lax.dot_general(a, b, (((1,), (1,)), ((), ())), preferred_element_type=F32)


def mm_tn(a, b):
    return lax.dot_general(a, b, (((0,), (0,)), ((), ())), preferred_element_type=F32)


def iota(shape, dim):
    return lax.broadcasted_iota(jnp.int32, shape, dim)


def whole(ref, start, size):
    piece = ref[:, :, start : start + size, :]
    return piece.reshape(GROUP * 2 * size, piece.shape[3])


def run_copies(copies):
    for copy in copies:
        copy.start()
    for copy in copies:
        copy.wait()


def placed(meta_ref, pieces, target, sem, at):
    core = meta_ref[META_CORE]
    near, far, across = (meta_ref[META_SLOT + i] for i in range(3))
    slots = ((near, core), (far, core), (across, core), (far, 1 - core), (near, 1 - core), (across, 1 - core))
    return [
        pltpu.make_async_copy(piece, target(slot, half), sem.at[at + i])
        for i, (piece, (slot, half)) in enumerate(zip(pieces, slots))
    ]


def load_first(meta_ref, own, pieces, w_ref, sem):
    me = meta_ref[META_SLOT + 3]
    copies = placed(meta_ref, pieces, lambda slot, half: w_ref.at[slot, half], sem, 0)
    at = len(copies)
    for half in range(2):
        for i, ref in enumerate(own):
            size = REL_HALF if i == 3 else HALF
            copies.append(
                pltpu.make_async_copy(
                    ref.at[pl.ds(half * size, size)], w_ref.at[me, half, pl.ds(i * HALF, size)], sem.at[at]
                )
            )
            at += 1
    return copies


def split_halves(meta_ref, value, keep_ref, send_ref, shard, rows, cols=slice(None)):
    half = value.shape[0] // 2
    low, high = value[:half].astype(LOW), value[half:].astype(LOW)
    first_core = meta_ref[META_CORE] == 0
    keep_ref[meta_ref[META_KEEP + shard], rows, cols] = jnp.where(first_core, low, high)
    send_ref[meta_ref[META_SEND + shard], rows, cols] = jnp.where(first_core, high, low)


def attend_forward_body(
    meta_ref, tok_ref, bucket_ref, own_q, own_k, own_v, own_rel, p0, p1, p2, p3, p4, p5,
    q_ref, k_ref, v_ref, pk_ref, pq_ref, relw_ref, probs_ref, ctx_ref,
    w_ref, sem,
):
    run_copies(load_first(meta_ref, (own_q, own_k, own_v, own_rel), (p0, p1, p2, p3, p4, p5), w_ref, sem))
    tok = tok_ref[...]
    rel = whole(w_ref, REL_AT, REL_HALF)
    pick = (bucket_ref[...] == iota((OFFS, OFFS), 1)).astype(LOW)
    relw = mm(pick, rel).astype(LOW)
    relw_ref[...] = relw
    w_query = whole(w_ref, 0, HALF)
    q_ref[...] = mm(tok, w_query).astype(LOW)
    pq_ref[...] = mm(relw, w_query).astype(LOW)
    w_key = whole(w_ref, HALF, HALF)
    k_ref[...] = mm(tok, w_key).astype(LOW)
    pk_ref[...] = mm(relw, w_key).astype(LOW)
    v_ref[...] = mm(tok, whole(w_ref, 2 * HALF, HALF)).astype(LOW)
    length = meta_ref[META_LENGTH]
    valid = iota((ROWS, ROWS), 1) < length
    side = iota((ROWS, 2 * HEAD_DIM), 1) // HEAD_DIM

    def pair_step(pair, carry):
        cols = pl.ds(pl.multiple_of(pair * 2 * HEAD_DIM, 2 * HEAD_DIM), 2 * HEAD_DIM)
        q_pair, k_pair, v_pair = q_ref[:, cols], k_ref[:, cols], v_ref[:, cols]
        pk_pair, pq_pair = pk_ref[:, cols], pq_ref[:, cols]
        zero = jnp.zeros_like(q_pair)
        contexts = []
        for h in range(2):
            mine = side == h
            q_head = jnp.where(mine, q_pair, zero)
            k_head = jnp.where(mine, k_pair, zero)
            content = mm_nt(q_head, k_pair)
            to_off = mm_nt(q_head, pk_pair)
            from_off = mm_nt(k_head, pq_pair)
            to_rel = pltpu.roll(to_off, ROWS + 1, 1, stride=1, stride_axis=0)[:, :ROWS]
            from_rel = pltpu.roll(from_off, ROWS + 1, 1, stride=1, stride_axis=0)[:, :ROWS]
            scores = (content + to_rel + from_rel.T) * SCALING
            scores = jnp.where(valid, scores, MASKED)
            top = jnp.max(scores, axis=1, keepdims=True)
            shifted = jnp.exp(scores - top)
            summed = jnp.sum(shifted, axis=1, keepdims=True)
            probs = (shifted * (1.0 / summed)).astype(LOW)
            probs_ref[2 * pair + h] = probs
            contexts.append(mm(probs, v_pair))
        ctx_ref[:, cols] = jnp.where(side == 0, contexts[0], contexts[1]).astype(LOW)
        return carry

    lax.fori_loop(0, PAIRS, pair_step, 0)


def attend_forward(meta, tok, bucket_column, own, pieces):
    shape = jax.ShapeDtypeStruct
    full, anywhere = pl.BlockSpec(memory_space=pltpu.VMEM), pl.BlockSpec(memory_space=pl.ANY)
    return pl.pallas_call(
        attend_forward_body,
        out_shape=(
            shape((ROWS, D), LOW), shape((ROWS, D), LOW), shape((ROWS, D), LOW),
            shape((OFFS, D), LOW), shape((OFFS, D), LOW), shape((OFFS, D), LOW),
            shape((HEADS, ROWS, ROWS), LOW), shape((ROWS, D), LOW),
        ),
        in_specs=[pl.BlockSpec(memory_space=pltpu.SMEM), full, full] + [anywhere] * 10,
        out_specs=(full,) * 8,
        scratch_shapes=[pltpu.VMEM((GROUP, 2, FIRST, D), LOW), pltpu.SemaphoreType.DMA((14,))],
        compiler_params=pltpu.CompilerParams(vmem_limit_bytes=28 * MIB),
        cost_estimate=pl.CostEstimate(flops=8_000_000_000, bytes_accessed=40_000_000, transcendentals=800_000),
        name="attend_forward",
    )(meta, tok, bucket_column, *own, *pieces)


def attend_backward_body(
    meta_ref, q_ref, k_ref, v_ref, pk_ref, pq_ref, relw_ref, probs_ref, gctx_ref, tok_ref, gres_ref, bucket_ref,
    own_q, own_k, own_v, own_rel, p0, p1, p2, p3, p4, p5,
    gtok_ref, keep_ref, send_ref,
    gq_ref, gk_ref, gv_ref, gpk_ref, gpq_ref, qr_ref, kr_ref, w_ref, sem,
):
    copies = load_first(meta_ref, (own_q, own_k, own_v, own_rel), (p0, p1, p2, p3, p4, p5), w_ref, sem)
    for copy in copies:
        copy.start()
    flip = (iota((ROWS, ROWS), 0) + iota((ROWS, ROWS), 1) == ROWS - 1).astype(LOW)
    qr_ref[...] = mm(flip, q_ref[...]).astype(LOW)
    kr_ref[...] = mm(flip, k_ref[...]).astype(LOW)
    side = iota((ROWS, 2 * HEAD_DIM), 1) // HEAD_DIM
    side_off = iota((OFFS, 2 * HEAD_DIM), 1) // HEAD_DIM
    blank = jnp.zeros((ROWS, OFFS - ROWS), F32)

    def pair_step(pair, carry):
        cols = pl.ds(pl.multiple_of(pair * 2 * HEAD_DIM, 2 * HEAD_DIM), 2 * HEAD_DIM)
        q_pair, k_pair, v_pair = q_ref[:, cols], k_ref[:, cols], v_ref[:, cols]
        pk_pair, pq_pair, gctx_pair = pk_ref[:, cols], pq_ref[:, cols], gctx_ref[:, cols]
        qr_pair, kr_pair = qr_ref[:, cols], kr_ref[:, cols]
        zero = jnp.zeros_like(q_pair)
        parts = []
        for h in range(2):
            gctx_head = jnp.where(side == h, gctx_pair, zero)
            grad_probs = mm_nt(gctx_head, v_pair)
            probs_low = probs_ref[2 * pair + h]
            probs = probs_low.astype(F32)
            inner = jnp.sum(probs * grad_probs, axis=1, keepdims=True)
            grad_scores = (probs * (grad_probs - inner)).astype(LOW)
            g_value = mm_tn(probs_low, gctx_pair)
            rows_back = mm(flip, grad_scores)
            cols_back = mm_nt(flip, grad_scores)
            to_off = pltpu.roll(jnp.concatenate([rows_back, blank], axis=1), 0, 1, stride=1, stride_axis=0).astype(LOW)
            from_off = pltpu.roll(jnp.concatenate([cols_back, blank], axis=1), 0, 1, stride=1, stride_axis=0).astype(LOW)
            g_query = mm(rows_back.astype(LOW), k_pair) + mm(to_off, pk_pair)
            g_key = mm(cols_back.astype(LOW), q_pair) + mm(from_off, pq_pair)
            g_pk = mm_tn(to_off, qr_pair)
            g_pq = mm_tn(from_off, kr_pair)
            parts.append((g_value, g_query, g_key, g_pk, g_pq))
        first, second = parts
        gv_ref[:, cols] = jnp.where(side == 0, first[0], second[0]).astype(LOW)
        gq_ref[:, cols] = (jnp.where(side == 0, first[1], second[1]) * SCALING).astype(LOW)
        gk_ref[:, cols] = (jnp.where(side == 0, first[2], second[2]) * SCALING).astype(LOW)
        gpk_ref[:, cols] = (jnp.where(side_off == 0, first[3], second[3]) * SCALING).astype(LOW)
        gpq_ref[:, cols] = (jnp.where(side_off == 0, first[4], second[4]) * SCALING).astype(LOW)
        return carry

    lax.fori_loop(0, PAIRS, pair_step, 0)
    for copy in copies:
        copy.wait()
    tok, relw = tok_ref[...], relw_ref[...]
    g_query = mm(flip, gq_ref[...]).astype(LOW)
    w_query = whole(w_ref, 0, HALF)
    g_tok = gres_ref[...] + mm_nt(g_query, w_query)
    g_rel = mm_nt(gpq_ref[...], w_query)

    def put(start, size, value):
        for shard in range(GROUP):
            rows = value[shard * 2 * size : (shard + 1) * 2 * size]
            split_halves(meta_ref, rows, keep_ref, send_ref, shard, slice(start, start + size))

    put(0, HALF, mm_tn(tok, g_query) + mm_tn(relw, gpq_ref[...]))
    g_key = mm(flip, gk_ref[...]).astype(LOW)
    w_key = whole(w_ref, HALF, HALF)
    g_tok = g_tok + mm_nt(g_key, w_key)
    g_rel = (g_rel + mm_nt(gpk_ref[...], w_key)).astype(LOW)
    put(HALF, HALF, mm_tn(tok, g_key) + mm_tn(relw, gpk_ref[...]))
    g_value = gv_ref[...]
    gtok_ref[...] = (g_tok + mm_nt(g_value, whole(w_ref, 2 * HALF, HALF))).astype(LOW)
    put(2 * HALF, HALF, mm_tn(tok, g_value))
    pick = (bucket_ref[...] == iota((OFFS, OFFS), 1)).astype(LOW)
    put(REL_AT, REL_HALF, mm_tn(pick, g_rel))


def attend_backward(meta, saved, gctx, tok, gres, bucket_column, own, pieces):
    shape = jax.ShapeDtypeStruct
    full, anywhere = pl.BlockSpec(memory_space=pltpu.VMEM), pl.BlockSpec(memory_space=pl.ANY)
    return pl.pallas_call(
        attend_backward_body,
        out_shape=(shape((ROWS, D), LOW), shape((GROUP, FIRST, D), LOW), shape((GROUP, FIRST, D), LOW)),
        in_specs=[pl.BlockSpec(memory_space=pltpu.SMEM)] + [full] * 11 + [anywhere] * 10,
        out_specs=(full,) * 3,
        scratch_shapes=[
            pltpu.VMEM((ROWS, D), LOW), pltpu.VMEM((ROWS, D), LOW), pltpu.VMEM((ROWS, D), LOW),
            pltpu.VMEM((OFFS, D), LOW), pltpu.VMEM((OFFS, D), LOW),
            pltpu.VMEM((ROWS, D), LOW), pltpu.VMEM((ROWS, D), LOW),
            pltpu.VMEM((GROUP, 2, FIRST, D), LOW), pltpu.SemaphoreType.DMA((14,)),
        ],
        compiler_params=pltpu.CompilerParams(vmem_limit_bytes=36 * MIB),
        cost_estimate=pl.CostEstimate(flops=12_000_000_000, bytes_accessed=60_000_000, transcendentals=0),
        name="attend_backward",
    )(meta, *saved, gctx, tok, gres, bucket_column, *own, *pieces)


def feed_body(
    meta_ref, tok_ref, ctx_ref, up_ref, own_outer, own_out, own_norm, own_inner,
    a0, a1, a2, a3, a4, a5, b0, b1, b2, b3, b4, b5,
    out_ref, gctx_ref, gres_ref, keep_ref, send_ref, keep_in_ref, send_in_ref,
    low_ref, act_ref, slope_ref, w_ref, in_ref, sem,
):
    me = meta_ref[META_SLOT + 3]
    copies = placed(meta_ref, (a0, a1, a2, a3, a4, a5), lambda slot, half: w_ref.at[slot, half], sem, 0)
    copies += placed(
        meta_ref, (b0, b1, b2, b3, b4, b5), lambda slot, half: in_ref.at[pl.ds(slot * PIECE + half * HALF, HALF)], sem, 6
    )
    copies.append(pltpu.make_async_copy(own_inner, in_ref.at[pl.ds(me * PIECE, PIECE)], sem.at[12]))
    copies.append(pltpu.make_async_copy(own_norm, w_ref.at[me, 0, pl.ds(NORM_AT, 16)], sem.at[13]))
    for half in range(2):
        copies.append(
            pltpu.make_async_copy(
                own_outer.at[pl.ds(half * (D // 2), D // 2)], w_ref.at[me, half, pl.ds(0, D // 2)], sem.at[14 + half]
            )
        )
        copies.append(
            pltpu.make_async_copy(
                own_out.at[pl.ds(half * HALF, HALF)], w_ref.at[me, half, pl.ds(OUT_AT, HALF)], sem.at[16 + half]
            )
        )
    run_copies(copies)
    length = meta_ref[META_LENGTH]
    mask = (iota((ROWS, 1), 0) < length).astype(F32)
    norm_rows = [w_ref[s, 0, NORM_AT : NORM_AT + 16, :].astype(F32)[:1] for s in range(GROUP)]
    gain_one, bias_one, gain_two, bias_two = (
        jnp.concatenate([row[:, i * PIECE : (i + 1) * PIECE] for row in norm_rows], axis=1) for i in range(4)
    )
    token = tok_ref[...].astype(F32)
    ctx = ctx_ref[...]
    w_out = whole(w_ref, OUT_AT, HALF)
    attn = mm(ctx, w_out)

    def norm(values):
        center = values - jnp.mean(values, axis=1, keepdims=True)
        inverse = lax.rsqrt(jnp.mean(center * center, axis=1, keepdims=True) + EPSILON)
        return center * inverse, inverse

    def norm_back(upstream, normed, inverse, gain):
        scaled = upstream * gain
        plain = jnp.mean(scaled, axis=1, keepdims=True)
        cross = jnp.mean(scaled * normed, axis=1, keepdims=True)
        return inverse * (scaled - plain - normed * cross)

    def total(values):
        return jnp.sum(values, axis=0, keepdims=True)

    normed_one, inverse_one = norm(token + attn)
    hidden_one = normed_one * gain_one + bias_one
    low_ref[...] = hidden_one.astype(LOW)

    def columns(c):
        return pl.ds(pl.multiple_of(c * D, D), D)

    def outer_rows(c):
        return w_ref[c, :, 0 : D // 2, :].reshape(D, D)

    def forward_step(c, ffn):
        inner = mm(low_ref[...], in_ref[:, columns(c)])
        cumulative = 0.5 * (1.0 + lax.erf(inner * 0.5**0.5))
        density = jnp.exp(-0.5 * inner * inner) * 0.3989422804014327
        act = (inner * cumulative).astype(LOW)
        act_ref[c] = act
        slope_ref[c] = cumulative + inner * density
        return ffn + mm(act, outer_rows(c))

    ffn = lax.fori_loop(0, GROUP, forward_step, jnp.zeros((ROWS, D), F32))
    normed_two, inverse_two = norm(hidden_one + ffn)
    layer = (normed_two * gain_two + bias_two) * mask
    out_ref[...] = layer.astype(LOW)
    squares = [token * token * mask, attn * attn * mask, ffn * ffn * mask, layer * layer]
    sums = [jnp.sum(total(s), axis=1, keepdims=True) for s in squares]
    grad_y = up_ref[...].astype(F32) * mask
    grad_gain_two = total(grad_y * normed_two)
    grad_bias_two = total(grad_y)
    grad_two = norm_back(grad_y, normed_two, inverse_two, gain_two)
    grad_ffn = grad_two.astype(LOW)

    def back_step(c, grad_hidden):
        grad_act = mm_nt(grad_ffn, outer_rows(c))
        grad_inner = (grad_act * slope_ref[c]).astype(LOW)
        split_halves(meta_ref, mm_tn(act_ref[c], grad_ffn), keep_ref, send_ref, c, slice(0, D // 2))
        grad_w = mm_tn(low_ref[...], grad_inner)
        for s in range(GROUP):
            rows = grad_w[s * PIECE : (s + 1) * PIECE]
            split_halves(meta_ref, rows, keep_in_ref, send_in_ref, s, slice(None), columns(c))
        return grad_hidden + mm_nt(grad_inner, in_ref[:, columns(c)])

    grad_hidden = lax.fori_loop(0, GROUP, back_step, grad_two)
    grad_gain_one = total(grad_hidden * normed_one)
    grad_bias_one = total(grad_hidden)
    grad_one = norm_back(grad_hidden, normed_one, inverse_one, gain_one)
    gres_ref[...] = grad_one
    grad_attn = grad_one.astype(LOW)
    grad_out = mm_tn(ctx, grad_attn)
    for s in range(GROUP):
        rows = grad_out[s * PIECE : (s + 1) * PIECE]
        split_halves(meta_ref, rows, keep_ref, send_ref, s, slice(OUT_AT, OUT_AT + HALF))
    gctx_ref[...] = mm_nt(grad_attn, w_out).astype(LOW)
    lane = iota((1, D), 1)
    stats = jnp.zeros((1, D), F32)
    for i, value in enumerate(sums):
        stats = jnp.where(lane == i, value, stats)
    low = stats - stats.astype(LOW).astype(F32)
    zeros = jnp.zeros((1, D), F32)
    norm_rows = (grad_gain_one, grad_bias_one, grad_gain_two, grad_bias_two)
    for s in range(GROUP):
        row = jnp.concatenate([r[:, s * PIECE : (s + 1) * PIECE] for r in norm_rows], axis=1)
        block = jnp.concatenate([row] + [zeros] * 15 + [stats, low] + [zeros] * 14, axis=0)
        split_halves(meta_ref, block, keep_ref, send_ref, s, slice(NORM_AT, NORM_AT + 16))


def feed(meta, tok, ctx, up, own, outer_pieces, inner_pieces):
    shape = jax.ShapeDtypeStruct
    full, anywhere = pl.BlockSpec(memory_space=pltpu.VMEM), pl.BlockSpec(memory_space=pl.ANY)
    block, wide = shape((GROUP, SECOND, D), LOW), shape((GROUP, HALF, WIDE), LOW)
    return pl.pallas_call(
        feed_body,
        out_shape=(shape((ROWS, D), LOW), shape((ROWS, D), LOW), shape((ROWS, D), F32), block, block, wide, wide),
        in_specs=[pl.BlockSpec(memory_space=pltpu.SMEM)] + [full] * 3 + [anywhere] * 16,
        out_specs=(full,) * 7,
        scratch_shapes=[
            pltpu.VMEM((ROWS, D), LOW), pltpu.VMEM((GROUP, ROWS, D), LOW), pltpu.VMEM((GROUP, ROWS, D), F32),
            pltpu.VMEM((GROUP, 2, SECOND, D), LOW), pltpu.VMEM((D, WIDE), LOW), pltpu.SemaphoreType.DMA((18,)),
        ],
        compiler_params=pltpu.CompilerParams(vmem_limit_bytes=48 * MIB),
        cost_estimate=pl.CostEstimate(flops=12_000_000_000, bytes_accessed=60_000_000, transcendentals=1_600_000),
        name="feed",
    )(meta, tok, ctx, up, *own, *outer_pieces, *inner_pieces)


def pairs_over(size, flips):
    return [(c, i, c, i ^ flips[c]) for c in range(2) for i in range(size)]


def hop(value, axis, flips):
    if axis == "shard":
        pairs = [(c * 4 + i, d * 4 + j) for c, i, d, j in pairs_over(4, flips)]
        return lax.ppermute(value, ("core", "shard"), pairs)
    pairs = [(i * 2 + c, j * 2 + d) for c, i, d, j in pairs_over(4, flips)]
    return lax.ppermute(value, (axis, "core"), pairs)


NEAR, FAR = (1, 3), (3, 1)


def swap(value):
    return lax.ppermute(value, "core", [(0, 1), (1, 0)])


def spread(half):
    near = hop(half, "shard", NEAR)
    far = hop(half, "shard", FAR)
    across = hop(near, "shard", FAR)
    return near, far, across, swap(near), swap(far), swap(across)


def add(*values):
    total = values[0].astype(F32)
    for value in values[1:]:
        total = total + value.astype(F32)
    return total.astype(LOW)


def reduce_over_all(keep, send):
    other = swap(send)
    first = hop(add(keep[:2], other[:2]), "shard", NEAR)
    second = hop(add(keep[2], other[2], first[0]), "shard", FAR)
    mine = add(keep[3], other[3], first[1], second)
    rows = mine.shape[0] // 2
    parts = []
    for part, order in ((mine[:rows], ("y", "z")), (mine[rows:], ("z", "y"))):
        for axis in order:
            for flips in (NEAR, FAR):
                part = add(part, hop(part, axis, flips))
        parts.append(part)
    mine = jnp.concatenate(parts, axis=0)
    return mine, swap(mine)


def arrange(lengths):
    slots = jnp.arange(GROUP, dtype=jnp.int32)
    longer = (lengths[None, :] > lengths[:, None]) | (lengths[None, :] == lengths[:, None]) & (
        slots[None, :] < slots[:, None]
    )
    dealing = jnp.sum(longer.astype(jnp.int32), axis=1)
    chosen = (dealing[None, :] == slots[:, None]).astype(jnp.int32)
    source_of = jnp.sum(chosen * slots[None, :], axis=1)
    return dealing, source_of


def shards(
    hidden, grad_out, lengths, bucket, w_query, w_key, w_value, w_out, w_inner, w_outer, rel_table,
    ln1_gain, ln1_bias, ln2_gain, ln2_bias,
):
    member = lax.axis_index("shard")
    dealing, source_of = arrange(lengths)
    both = jnp.concatenate([jnp.take(hidden, source_of, axis=0), jnp.take(grad_out, source_of, axis=0)], axis=2)
    arrived = lax.all_to_all(both, "shard", split_axis=0, concat_axis=1, tiled=True)[0]
    tok, up = arrived[:, :D], arrived[:, D:]
    core = lax.axis_index("core")
    length = jnp.sum(jnp.where(dealing == member, lengths, 0))
    near, far = jnp.where(core == 0, 1, 3), jnp.where(core == 0, 3, 1)
    slots = jnp.stack([member ^ near, member ^ far, member ^ 2, member])
    shard_ids = jnp.arange(GROUP, dtype=jnp.int32) ^ member
    table = jnp.array([[3, 1, 0, 2], [3, 2, 0, 1]], jnp.int32)
    keep_at = jnp.take(jnp.take(table, core, axis=0), shard_ids)
    send_at = jnp.take(jnp.take(table, 1 - core, axis=0), shard_ids)
    meta = jnp.concatenate([jnp.stack([length, core]), slots, keep_at, send_at]).astype(jnp.int32)

    def half_of(matrix):
        size = matrix.shape[0] // 2
        return lax.dynamic_slice_in_dim(matrix, core * size, size, 0)

    norm_block = jnp.concatenate(
        [jnp.concatenate([ln1_gain, ln1_bias, ln2_gain, ln2_bias])[None], jnp.zeros((15, D), LOW)], axis=0
    )
    own_first = (w_query, w_key, w_value, rel_table)
    first = spread(jnp.concatenate([half_of(matrix) for matrix in own_first], axis=0))
    outer = spread(jnp.concatenate([half_of(w_outer), half_of(w_out), norm_block], axis=0))
    inner = spread(half_of(w_inner))
    bucket_column = jnp.concatenate([bucket[::-1], jnp.full((1,), -1, jnp.int32)])[:, None]
    *saved, ctx = attend_forward(meta, tok, bucket_column, own_first, first)
    out, gctx, gres, keep, send, keep_in, send_in = feed(
        meta, tok, ctx, up, (w_outer, w_out, norm_block, w_inner), outer, inner
    )
    gtok, keep_first, send_first = attend_backward(meta, saved, gctx, tok, gres, bucket_column, own_first, first)

    def whole_shard(halves):
        mine, other = (half.astype(F32) for half in halves)
        return jnp.where(core == 0, mine, other), jnp.where(core == 0, other, mine)

    def rows(halves, start, size):
        return jnp.concatenate([half[start : start + size] for half in halves], axis=0)

    two = whole_shard(reduce_over_all(keep, send))
    wide = whole_shard(reduce_over_all(keep_in, send_in))
    one = whole_shard(reduce_over_all(keep_first, send_first))
    returned = lax.all_to_all(
        jnp.concatenate([out, gtok], axis=1)[None], "shard", split_axis=1, concat_axis=0, tiled=True
    )
    returned = jnp.take(returned, dealing, axis=0)
    norm_sums = two[0][NORM_AT].reshape(GROUP, PIECE)
    stats = two[1][NORM_AT, :GROUP] + two[1][NORM_AT + 1, :GROUP]
    return (
        returned[:, :, :D],
        returned[:, :, D:],
        rows(one, 0, HALF),
        rows(one, HALF, HALF),
        rows(one, 2 * HALF, HALF),
        rows(two, OUT_AT, HALF),
        rows(wide, 0, HALF),
        rows(two, 0, D // 2),
        rows(one, REL_AT, REL_HALF),
        norm_sums[0],
        norm_sums[1],
        norm_sums[2],
        norm_sums[3],
        jnp.sqrt(stats / (TOKENS * D)),
    )


def solution(mesh):
    split = Mesh(mesh.devices.reshape(4, 4, 2, 4), ("y", "z", "core", "shard"))
    rep = ("y", "z", "core")
    rows, vector = P("shard", None), P("shard")
    batch = P(rep, "shard", None)
    return jax.shard_map(
        shards,
        mesh=split,
        in_specs=(batch, batch, P(rep), P(), *(rows,) * 7, *(vector,) * 4),
        out_specs=(batch, batch, *(rows,) * 7, *(vector,) * 4, P()),
        check_vma=False,
    )
```

time: 969 us -> 312 us (0.32)
  matrix products: 302 us -> 0 us
  blocking collectives: 205 us -> 0 us
  local copies, waits for them, and re-layouts: 231 us -> 26.6 us
  starting transfers between devices: 7.87 us -> 78.4 us
  Pallas kernels: 0 us -> 58.1 us
  waiting for transfers between devices: 145 us -> 104 us
  between operations: 17.7 us -> 1.6 us
    dot_general x228 -> x0, matrix products: 302 us -> none  [the longest x24 28.2 us: head_scores(): jnp.einsum('me,oe->mo', key_head, posq_wide, preferred_element_type=jnp.f...]
    psum x2 -> x0, blocking collectives: 167 us -> none  [the longest x1 112 us: shards(): lax.psum((heads_join(head_grads[3]), heads_join(head_grads[4]), squares),...]
    ppermute x0 -> x54, waiting for transfers between devices: none -> 101 us  [the longest x15 66.2 us: hop(): return lax.ppermute(value, ('core', 'shard'), pairs)]
    while x276 -> x0, local copies, waits for them, and re-layouts: 79.3 us -> none
    ppermute x0 -> x54, starting transfers between devices: none -> 70.3 us  [the longest x24 28 us: hop(): return lax.ppermute(value, (axis, 'core'), pairs)]
    all_gather x2 -> x0, waiting for transfers between devices: 63.8 us -> none  [the longest x1 63.7 us: sent_together(): lax.all_gather(both, axis, axis=dim, tiled=True)]
    pallas_call x0 -> x3, Pallas kernels: none -> 58.1 us  [the longest x1 22.3 us: feed(): pl.pallas_call(feed_body, out_shape=(shape((ROWS, D), LOW), shape((ROWS,...]
    reduce_scatter x6 -> x0, waiting for transfers between devices: 57.6 us -> none  [the longest x1 53 us: shards(): lax.psum_scatter(grad_w_inner.astype(jnp.bfloat16), 'shard', scatter_dime...]
  transfers between devices with their start and end apart: 11 -> 56, of which waited for: 4 -> 22; matrix products, arithmetic and copies ran while one was open for 56% -> 18% of each run, Pallas kernels for 0% -> 5%
where the time goes in v1:
time: 312 us; the launch traced here: 306 us
  waiting for transfers between devices  104 us (33%)
  starting transfers between devices  78.4 us (25%)
  Pallas kernels  58.1 us (19%)
  other arithmetic  37.5 us (12%)
  local copies, waits for them, and re-layouts  26.6 us (9%)
    ppermute x15, waiting for transfers between devices, hop(): return lax.ppermute(value, ('core', 'shard'), pairs)  66.2 us
    ppermute x24, waiting for transfers between devices, hop(): return lax.ppermute(value, (axis, 'core'), pairs)  35 us
    ppermute x24, starting transfers between devices, hop(): return lax.ppermute(value, (axis, 'core'), pairs)  28 us
    ppermute x15, starting transfers between devices, swap(): return lax.ppermute(value, 'core', [(0, 1), (1, 0)])  26.5 us
    pallas_call x1, Pallas kernels, feed(): pl.pallas_call(feed_body, out_shape=(shape((ROWS, D), LOW), shape((ROWS,...  22.3 us
    pallas_call x1, Pallas kernels, attend_backward(): pl.pallas_call(attend_backward_body, out_shape=(shape((ROWS, D), LOW), sh...  20.8 us
    convert_element_type x30, other arithmetic, add(): return total.astype(LOW)  18.2 us
    ppermute x15, starting transfers between devices, hop(): return lax.ppermute(value, ('core', 'shard'), pairs)  15.9 us
  transfers between devices with their start and end apart: 56, of which 22 were waited for; matrix products, arithmetic and copies ran while one was open for 18% of the time, Pallas kernels for 5%

profile of v1, /device:TPU:17, one launch (start us, length us, event | category | flops | bytes accessed | tf_op | source)
XLA Modules:
  0.0 305.8 jit_solution(10817741919933772535)
XLA Ops:
  21.6 24.9 %collective-permute-done.12.b0 = bf16[96,3072]{1,0:T(8,128)(2,1)S(1)} collective-permute-done((bf16[96,3072]{1,0:T(8,128)(2,1)}, bf16[96,3072]{1,0:T(8,128)(2,1)S(1)}, u32[]{:S(2)}, u32[]{:S(2)}) %collective-permute-start.12) | collective-permute-done | bytes 589856 | tf_op jit(solution)/shard_map/ppermute | solution.py:403
  51.5 4.3 %all-to-all-start = ((bf16[4,64,1536]{2,1,0:T(8,128)(2,1)}), bf16[4,64,1536]{2,1,0:T(8,128)(2,1)}, u32[]{:S(2)}, u32[]{:S(2)}) async-start(bf16[4,64,1536]{2,1,0:T(8,128)(2,1)} %pad_maximum_fusion.2), calls=%async_computation | async-start | bytes 1572864 | tf_op jit(solution)/shard_map/all_to_all | solution.py:463
  57.4 3.6 %collective-permute-start.4 = (bf16[352,768]{1,0:T(8,128)(2,1)}, bf16[352,768]{1,0:T(8,128)(2,1)}, u32[]{:S(2)}, u32[]{:S(2)}) collective-permute-start(bf16[352,768]{1,0:T(8,128)(2,1)} %copy-done.10), channel_id=1, source_target_pairs={{0,4},{4,0},{1,5},{5,1},{2,6},{6,2},{3,7},{7,3},{8,12},{12,8},{9,1... | collective-permute-start | bytes 1622024 | tf_op jit(solution)/shard_map/ppermute | solution.py:412
  64.2 13.7 %collective-permute-done.14.b2 = bf16[96,3072]{1,0:T(8,128)(2,1)} collective-permute-done((bf16[96,3072]{1,0:T(8,128)(2,1)S(1)}, bf16[96,3072]{1,0:T(8,128)(2,1)}, u32[]{:S(2)}, u32[]{:S(2)}) %collective-permute-start.14) | collective-permute-done | bytes 589856 | tf_op jit(solution)/shard_map/ppermute | solution.py:403
  81.6 15.0 %attend_forward.1 = (bf16[256,768]{1,0:T(8,128)(2,1)S(1)}, bf16[256,768]{1,0:T(8,128)(2,1)S(1)}, bf16[256,768]{1,0:T(8,128)(2,1)S(1)}, bf16[512,768]{1,0:T(8,128...) custom-call(s32[14]{0:T(128)S(1)} %concatenate.55.meta_ref, ...), custom_call_target="tpu_custom_call" | custom-call | flops 8000000000 | bytes 40000000 | tf_op jit(solution)/shard_map/attend_forward/pallas_call | solution.py:151
  96.7 22.3 %feed.1 = (bf16[256,768]{1,0:T(8,128)(2,1)S(1)}, bf16[256,768]{1,0:T(8,128)(2,1)S(1)}, f32[256,768]{1,0:T(8,128)}, bf16[4,496,768]{2,1,0:T(8,128)(2,1)}, bf16[4,...) custom-call(s32[14]{0:T(128)S(1)} %concatenate.55.meta_ref, ...), custom_call_target="tpu_custom_call" | custom-call | flops 12000000000 | bytes 60000000 | tf_op jit(solution)/shard_map/feed/pallas_call | solution.py:381
  120.1 20.8 %attend_backward.1 = (bf16[256,768]{1,0:T(8,128)(2,1)S(1)}, bf16[4,352,768]{2,1,0:T(8,128)(2,1)S(1)}, bf16[4,352,768]{2,1,0:T(8,128)(2,1)}) custom-call(s32[14]{0:T(128)S(1)} %concatenate.55.meta_ref, bf16[256,768]{1,0:T(8,128)(2,1)S(1)} %get-tuple-element.37.q_ref, bf16[256,768]{1,0:T(8,128)(2,1)S(1)} %get-tuple-element.38.k_ref, ...), custom_call_target="tpu_custom_call" | custom-call | flops 12000000000 | bytes 60000000 | tf_op jit(solution)/shard_map/attend_backward/pallas_call | solution.py:245
  144.5 6.4 %reduce = bf16[256,1536]{1,0:T(8,128)(2,1)S(1)} reduce(bf16[256,1,1536]{2,1,0:T(2,128)(2,1)} %bitcast.48, bf16[]{:T(256)} %broadcast.158), dimensions={1}, to_apply=%bitcast.47.reduce_sub_computation | reduce | bytes 1572866
  152.3 3.7 %all-to-all-start.1 = ((bf16[4,2,49152]{2,1,0:T(2,128)(2,1)}), bf16[4,2,49152]{2,1,0:T(2,128)(2,1)S(1)}, u32[]{:S(2)}, u32[]{:S(2)}) async-start(bf16[4,2,49152]{2,1,0:T(2,128)(2,1)} %reshape.209), calls=%async_computation.1 | async-start | bytes 1572864 | tf_op jit(solution)/shard_map/all_to_all | solution.py:503
  159.4 3.3 %collective-permute-start.19 = (bf16[2,352,768]{2,1,0:T(8,128)(2,1)}, bf16[2,352,768]{2,1,0:T(8,128)(2,1)}, u32[]{:S(2)}, u32[]{:S(2)}) collective-permute-start(bf16[2,352,768]{2,1,0:T(8,128)(2,1)} %add_convert_fusion.2), channel_id=1, source_target_pairs={{0,1},{1,0},{2,3},{3,2},{4,7},{5,6},{6,5},{7,4},{8,9},{9,8},{10,11... | collective-permute-start | bytes 3244040 | tf_op jit(solution)/shard_map/ppermute | solution.py:403
  162.7 2.7 add_convert_fusion.1
  175.0 5.0 %collective-permute-done.19 = bf16[2,352,768]{2,1,0:T(8,128)(2,1)} collective-permute-done((bf16[2,352,768]{2,1,0:T(8,128)(2,1)}, bf16[2,352,768]{2,1,0:T(8,128)(2,1)}, u32[]{:S(2)}, u32[]{:S(2)}) %collective-permute-start.19) | collective-permute-done | bytes 1081376 | tf_op jit(solution)/shard_map/ppermute | solution.py:403
  181.7 16.7 %collective-permute-done.43 = bf16[2,96,3072]{2,1,0:T(8,128)(2,1)} collective-permute-done((bf16[2,96,3072]{2,1,0:T(8,128)(2,1)}, bf16[2,96,3072]{2,1,0:T(8,128)(2,1)}, u32[]{:S(2)}, u32[]{:S(2)}) %collective-permute-start.43) | collective-permute-done | bytes 1179680 | tf_op jit(solution)/shard_map/ppermute | solution.py:403
  202.0 3.8 %collective-permute-start.25 = (bf16[176,768]{1,0:T(8,128)(2,1)S(1)}, bf16[176,768]{1,0:T(8,128)(2,1)S(1)}, u32[]{:S(2)}, u32[]{:S(2)}) collective-permute-start(bf16[176,768]{1,0:T(8,128)(2,1)S(1)} %get-tuple-element.95), channel_id=1, source_target_pairs={{0,8},{8,0},{16,24},{24,16},{4,28},{12,20},{20,12},{28,4},{1,9},{9... | collective-permute-start | bytes 811016 | tf_op jit(solution)/shard_map/ppermute | solution.py:405
  214.5 2.7 collective-permute-start.49
  224.3 3.2 %collective-permute-done.31 = bf16[2,496,768]{2,1,0:T(8,128)(2,1)S(1)} collective-permute-done((bf16[2,496,768]{2,1,0:T(8,128)(2,1)S(1)}, bf16[2,496,768]{2,1,0:T(8,128)(2,1)S(1)}, u32[]{:S(2)}, u32[]{:S(2)}) %collective-permute-start.31) | collective-permute-done | bytes 1523744 | tf_op jit(solution)/shard_map/ppermute | solution.py:403
  236.1 7.5 %collective-permute-start.29 = (bf16[352,768]{1,0:T(8,128)(2,1)S(1)}, bf16[352,768]{1,0:T(8,128)(2,1)S(1)}, u32[]{:S(2)}, u32[]{:S(2)}) collective-permute-start(bf16[352,768]{1,0:T(8,128)(2,1)S(1)} %pad_maximum_fusion.10), channel_id=1, source_target_pairs={{0,4},{4,0},{1,5},{5,1},{2,6},{6,2},{3,7},{7,3},{8,12},{12,8},{9,1... | collective-permute-start | bytes 1622024 | tf_op jit(solution)/shard_map/ppermute | solution.py:412
  244.5 5.1 %collective-permute-done.52 = bf16[48,3072]{1,0:T(8,128)(2,1)S(1)} collective-permute-done((bf16[48,3072]{1,0:T(8,128)(2,1)S(1)}, bf16[48,3072]{1,0:T(8,128)(2,1)S(1)}, u32[]{:S(2)}, u32[]{:S(2)}) %collective-permute-start.52) | collective-permute-done | bytes 294944 | tf_op jit(solution)/shard_map/ppermute | solution.py:405
  256.1 2.9 collective-permute-done.33
  262.1 5.1 %collective-permute-done.38 = bf16[248,768]{1,0:T(8,128)(2,1)S(1)} collective-permute-done((bf16[248,768]{1,0:T(8,128)(2,1)S(1)}, bf16[248,768]{1,0:T(8,128)(2,1)S(1)}, u32[]{:S(2)}, u32[]{:S(2)}) %collective-permute-start.38) | collective-permute-done | bytes 380960 | tf_op jit(solution)/shard_map/ppermute | solution.py:405
  272.3 5.9 %collective-permute-done.39 = bf16[248,768]{1,0:T(8,128)(2,1)S(1)} collective-permute-done((bf16[248,768]{1,0:T(8,128)(2,1)S(1)}, bf16[248,768]{1,0:T(8,128)(2,1)S(1)}, u32[]{:S(2)}, u32[]{:S(2)}) %collective-permute-start.39) | collective-permute-done | bytes 380960 | tf_op jit(solution)/shard_map/ppermute | solution.py:405
  281.1 4.1 %collective-permute-done.40 = bf16[248,768]{1,0:T(8,128)(2,1)S(1)} collective-permute-done((bf16[248,768]{1,0:T(8,128)(2,1)S(1)}, bf16[248,768]{1,0:T(8,128)(2,1)S(1)}, u32[]{:S(2)}, u32[]{:S(2)}) %collective-permute-start.40) | collective-permute-done | bytes 380960 | tf_op jit(solution)/shard_map/ppermute | solution.py:405
  285.2 4.8 %collective-permute-done.36 = bf16[248,768]{1,0:T(8,128)(2,1)S(1)} collective-permute-done((bf16[248,768]{1,0:T(8,128)(2,1)S(1)}, bf16[248,768]{1,0:T(8,128)(2,1)S(1)}, u32[]{:S(2)}, u32[]{:S(2)}) %collective-permute-start.36) | collective-permute-done | bytes 380960 | tf_op jit(solution)/shard_map/ppermute | solution.py:405
  290.2 9.5 %collective-permute-start.41 = (bf16[496,768]{1,0:T(8,128)(2,1)S(1)}, bf16[496,768]{1,0:T(8,128)(2,1)S(1)}, u32[]{:S(2)}, u32[]{:S(2)}) collective-permute-start(bf16[496,768]{1,0:T(8,128)(2,1)S(1)} %pad_maximum_fusion.3), channel_id=1, source_target_pairs={{0,4},{4,0},{1,5},{5,1},{2,6},{6,2},{3,7},{7,3},{8,12},{12,8},{9,1... | collective-permute-start | bytes 2285576 | tf_op jit(solution)/shard_map/ppermute | solution.py:412
  (239 shorter events, 107.3 us)
Async XLA Ops:
  9.4 39.0 %collective-permute-start.6 = (bf16[496,768]{1,0:T(8,128)(2,1)}, bf16[496,768]{1,0:T(8,128)(2,1)}, u32[]{:S(2)}, u32[]{:S(2)}) collective-permute-start(bf16[496,768]{1,0:T(8,128)(2,1)} %maximum_maximum_fusion), channel_id=1, source_target_pairs={{0,1},{1,0},{2,3},{3,2},{4,7},{5,6},{6,5},{7,4},{8,9},{9,8},{10,11... | collective-permute-start | bytes 2285576 | tf_op jit(solution)/shard_map/ppermute | solution.py:403
  10.2 47.2 %collective-permute-start.7 = (bf16[496,768]{1,0:T(8,128)(2,1)}, bf16[496,768]{1,0:T(8,128)(2,1)}, u32[]{:S(2)}, u32[]{:S(2)}) collective-permute-start(bf16[496,768]{1,0:T(8,128)(2,1)} %maximum_maximum_fusion), channel_id=1, source_target_pairs={{0,3},{1,2},{2,1},{3,0},{4,5},{5,4},{6,7},{7,6},{8,11},{9,10},{10,... | collective-permute-start | bytes 2285576 | tf_op jit(solution)/shard_map/ppermute | solution.py:403
  12.8 33.7 %collective-permute-start.12 = (bf16[96,3072]{1,0:T(8,128)(2,1)}, bf16[96,3072]{1,0:T(8,128)(2,1)S(1)}, u32[]{:S(2)}, u32[]{:S(2)}) collective-permute-start(bf16[96,3072]{1,0:T(8,128)(2,1)} %constant_dynamic-slice_fusion.2), channel_id=1, source_target_pairs={{0,1},{1,0},{2,3},{3,2},{4,7},{5,6},{6,5},{7,4},{8,9},{9,8},{10,11... | collective-permute-start | bytes 1769480 | tf_op jit(solution)/shard_map/ppermute | solution.py:403
  17.5 38.4 %collective-permute-start.13 = (bf16[96,3072]{1,0:T(8,128)(2,1)}, bf16[96,3072]{1,0:T(8,128)(2,1)S(1)}, u32[]{:S(2)}, u32[]{:S(2)}) collective-permute-start(bf16[96,3072]{1,0:T(8,128)(2,1)} %constant_dynamic-slice_fusion.2), channel_id=1, source_target_pairs={{0,3},{1,2},{2,1},{3,0},{4,5},{5,4},{6,7},{7,6},{8,11},{9,10},{10,... | collective-permute-start | bytes 1769480 | tf_op jit(solution)/shard_map/ppermute | solution.py:403
  21.6 40.9 %collective-permute-start.2 = (bf16[352,768]{1,0:T(8,128)(2,1)S(1)}, bf16[352,768]{1,0:T(8,128)(2,1)}, u32[]{:S(2)}, u32[]{:S(2)}) collective-permute-start(bf16[352,768]{1,0:T(8,128)(2,1)S(1)} %collective-permute-done.p0), channel_id=1, source_target_pairs={{0,3},{1,2},{2,1},{3,0},{4,5},{5,4},{6,7},{7,6},{8,11},{9,10},{10,... | collective-permute-start | bytes 1622024 | tf_op jit(solution)/shard_map/ppermute | solution.py:403
  48.4 29.9 %collective-permute-start.8 = (bf16[496,768]{1,0:T(8,128)(2,1)}, bf16[496,768]{1,0:T(8,128)(2,1)}, u32[]{:S(2)}, u32[]{:S(2)}) collective-permute-start(bf16[496,768]{1,0:T(8,128)(2,1)} %collective-permute-done.6.a0), channel_id=1, source_target_pairs={{0,3},{1,2},{2,1},{3,0},{4,5},{5,4},{6,7},{7,6},{8,11},{9,10},{10,... | collective-permute-start | bytes 2285576 | tf_op jit(solution)/shard_map/ppermute | solution.py:403
  51.5 27.0 %all-to-all-start = ((bf16[4,64,1536]{2,1,0:T(8,128)(2,1)}), bf16[4,64,1536]{2,1,0:T(8,128)(2,1)}, u32[]{:S(2)}, u32[]{:S(2)}) async-start(bf16[4,64,1536]{2,1,0:T(8,128)(2,1)} %pad_maximum_fusion.2), calls=%async_computation | async-start | bytes 1572864 | tf_op jit(solution)/shard_map/all_to_all | solution.py:463
  55.9 22.1 %collective-permute-start.14 = (bf16[96,3072]{1,0:T(8,128)(2,1)S(1)}, bf16[96,3072]{1,0:T(8,128)(2,1)}, u32[]{:S(2)}, u32[]{:S(2)}) collective-permute-start(bf16[96,3072]{1,0:T(8,128)(2,1)S(1)} %collective-permute-done.12.b0), channel_id=1, source_target_pairs={{0,3},{1,2},{2,1},{3,0},{4,5},{5,4},{6,7},{7,6},{8,11},{9,10},{10,... | collective-permute-start | bytes 1769480 | tf_op jit(solution)/shard_map/ppermute | solution.py:403
  62.5 17.2 %collective-permute-start.15 = (bf16[96,3072]{1,0:T(8,128)(2,1)S(1)}, bf16[96,3072]{1,0:T(8,128)(2,1)}, u32[]{:S(2)}, u32[]{:S(2)}) collective-permute-start(bf16[96,3072]{1,0:T(8,128)(2,1)S(1)} %collective-permute-done.12.b0), channel_id=1, source_target_pairs={{0,4},{4,0},{1,5},{5,1},{2,6},{6,2},{3,7},{7,3},{8,12},{12,8},{9,1... | collective-permute-start | bytes 1769480 | tf_op jit(solution)/shard_map/ppermute | solution.py:412
  62.5 17.7 %collective-permute-start.5 = (bf16[352,768]{1,0:T(8,128)(2,1)}, bf16[352,768]{1,0:T(8,128)(2,1)}, u32[]{:S(2)}, u32[]{:S(2)}) collective-permute-start(bf16[352,768]{1,0:T(8,128)(2,1)} %collective-permute-done.2.p2), channel_id=1, source_target_pairs={{0,4},{4,0},{1,5},{5,1},{2,6},{6,2},{3,7},{7,3},{8,12},{12,8},{9,1... | collective-permute-start | bytes 1622024 | tf_op jit(solution)/shard_map/ppermute | solution.py:412
  64.0 32.6 %collective-permute-start.9 = (bf16[496,768]{1,0:T(8,128)(2,1)}, bf16[496,768]{1,0:T(8,128)(2,1)}, u32[]{:S(2)}, u32[]{:S(2)}) collective-permute-start(bf16[496,768]{1,0:T(8,128)(2,1)} %collective-permute-done.6.a0), channel_id=1, source_target_pairs={{0,4},{4,0},{1,5},{5,1},{2,6},{6,2},{3,7},{7,3},{8,12},{12,8},{9,1... | collective-permute-start | bytes 2285576 | tf_op jit(solution)/shard_map/ppermute | solution.py:412
  77.9 18.7 %collective-permute-start.10 = (bf16[496,768]{1,0:T(8,128)(2,1)}, bf16[496,768]{1,0:T(8,128)(2,1)}, u32[]{:S(2)}, u32[]{:S(2)}) collective-permute-start(bf16[496,768]{1,0:T(8,128)(2,1)} %collective-permute-done.7.a1), channel_id=1, source_target_pairs={{0,4},{4,0},{1,5},{5,1},{2,6},{6,2},{3,7},{7,3},{8,12},{12,8},{9,1... | collective-permute-start | bytes 2285576 | tf_op jit(solution)/shard_map/ppermute | solution.py:412
  78.4 18.3 %collective-permute-start.11 = (bf16[496,768]{1,0:T(8,128)(2,1)}, bf16[496,768]{1,0:T(8,128)(2,1)}, u32[]{:S(2)}, u32[]{:S(2)}) collective-permute-start(bf16[496,768]{1,0:T(8,128)(2,1)} %collective-permute-done.8.a2), channel_id=1, source_target_pairs={{0,4},{4,0},{1,5},{5,1},{2,6},{6,2},{3,7},{7,3},{8,12},{12,8},{9,1... | collective-permute-start | bytes 2285576 | tf_op jit(solution)/shard_map/ppermute | solution.py:412
  79.7 16.9 %collective-permute-start.16 = (bf16[96,3072]{1,0:T(8,128)(2,1)S(1)}, bf16[96,3072]{1,0:T(8,128)(2,1)S(1)}, u32[]{:S(2)}, u32[]{:S(2)}) collective-permute-start(bf16[96,3072]{1,0:T(8,128)(2,1)S(1)} %collective-permute-done.13.b1), channel_id=1, source_target_pairs={{0,4},{4,0},{1,5},{5,1},{2,6},{6,2},{3,7},{7,3},{8,12},{12,8},{9,1... | collective-permute-start | bytes 1769480 | tf_op jit(solution)/shard_map/ppermute | solution.py:412
  80.2 16.4 %collective-permute-start.17 = (bf16[96,3072]{1,0:T(8,128)(2,1)}, bf16[96,3072]{1,0:T(8,128)(2,1)S(1)}, u32[]{:S(2)}, u32[]{:S(2)}) collective-permute-start(bf16[96,3072]{1,0:T(8,128)(2,1)} %collective-permute-done.14.b2), channel_id=1, source_target_pairs={{0,4},{4,0},{1,5},{5,1},{2,6},{6,2},{3,7},{7,3},{8,12},{12,8},{9,1... | collective-permute-start | bytes 1769480 | tf_op jit(solution)/shard_map/ppermute | solution.py:412
  141.4 21.3 %collective-permute-start.42 = (bf16[4,96,3072]{2,1,0:T(8,128)(2,1)}, bf16[4,96,3072]{2,1,0:T(8,128)(2,1)}, u32[]{:S(2)}, u32[]{:S(2)}) collective-permute-start(bf16[4,96,3072]{2,1,0:T(8,128)(2,1)} %get-tuple-element.52), channel_id=1, source_target_pairs={{0,4},{4,0},{1,5},{5,1},{2,6},{6,2},{3,7},{7,3},{8,12},{12,8},{9,1... | collective-permute-start | bytes 7077896 | tf_op jit(solution)/shard_map/ppermute | solution.py:412
  156.0 49.7 %collective-permute-start.30 = (bf16[4,496,768]{2,1,0:T(8,128)(2,1)}, bf16[4,496,768]{2,1,0:T(8,128)(2,1)}, u32[]{:S(2)}, u32[]{:S(2)}) collective-permute-start(bf16[4,496,768]{2,1,0:T(8,128)(2,1)} %get-tuple-element.50), channel_id=1, source_target_pairs={{0,4},{4,0},{1,5},{5,1},{2,6},{6,2},{3,7},{7,3},{8,12},{12,8},{9,1... | collective-permute-start | bytes 9142280 | tf_op jit(solution)/shard_map/ppermute | solution.py:412
  159.4 20.6 %collective-permute-start.19 = (bf16[2,352,768]{2,1,0:T(8,128)(2,1)}, bf16[2,352,768]{2,1,0:T(8,128)(2,1)}, u32[]{:S(2)}, u32[]{:S(2)}) collective-permute-start(bf16[2,352,768]{2,1,0:T(8,128)(2,1)} %add_convert_fusion.2), channel_id=1, source_target_pairs={{0,1},{1,0},{2,3},{3,2},{4,7},{5,6},{6,5},{7,4},{8,9},{9,8},{10,11... | collective-permute-start | bytes 3244040 | tf_op jit(solution)/shard_map/ppermute | solution.py:403
  165.4 33.0 %collective-permute-start.43 = (bf16[2,96,3072]{2,1,0:T(8,128)(2,1)}, bf16[2,96,3072]{2,1,0:T(8,128)(2,1)}, u32[]{:S(2)}, u32[]{:S(2)}) collective-permute-start(bf16[2,96,3072]{2,1,0:T(8,128)(2,1)} %add_convert_fusion.1), channel_id=1, source_target_pairs={{0,1},{1,0},{2,3},{3,2},{4,7},{5,6},{6,5},{7,4},{8,9},{9,8},{10,11... | collective-permute-start | bytes 3538952 | tf_op jit(solution)/shard_map/ppermute | solution.py:403
  181.4 18.6 %collective-permute-start.20 = (bf16[352,768]{1,0:T(8,128)(2,1)S(1)}, bf16[352,768]{1,0:T(8,128)(2,1)S(1)}, u32[]{:S(2)}, u32[]{:S(2)}) collective-permute-start(bf16[352,768]{1,0:T(8,128)(2,1)S(1)} %fusion.5), channel_id=1, source_target_pairs={{0,3},{1,2},{2,1},{3,0},{4,5},{5,4},{6,7},{7,6},{8,11},{9,10},{10,... | collective-permute-start | bytes 1622024 | tf_op jit(solution)/shard_map/ppermute | solution.py:403
  207.5 20.0 %collective-permute-start.31 = (bf16[2,496,768]{2,1,0:T(8,128)(2,1)S(1)}, bf16[2,496,768]{2,1,0:T(8,128)(2,1)S(1)}, u32[]{:S(2)}, u32[]{:S(2)}) collective-permute-start(bf16[2,496,768]{2,1,0:T(8,128)(2,1)S(1)} %add_convert_fusion), channel_id=1, source_target_pairs={{0,1},{1,0},{2,3},{3,2},{4,7},{5,6},{6,5},{7,4},{8,9},{9,8},{10,11... | collective-permute-start | bytes 4571144 | tf_op jit(solution)/shard_map/ppermute | solution.py:403
  229.0 21.5 %collective-permute-start.32 = (bf16[496,768]{1,0:T(8,128)(2,1)S(1)}, bf16[496,768]{1,0:T(8,128)(2,1)S(1)}, u32[]{:S(2)}, u32[]{:S(2)}) collective-permute-start(bf16[496,768]{1,0:T(8,128)(2,1)S(1)} %fusion.3), channel_id=1, source_target_pairs={{0,3},{1,2},{2,1},{3,0},{4,5},{5,4},{6,7},{7,6},{8,11},{9,10},{10,... | collective-permute-start | bytes 2285576 | tf_op jit(solution)/shard_map/ppermute | solution.py:403
  236.1 19.8 %collective-permute-start.29 = (bf16[352,768]{1,0:T(8,128)(2,1)S(1)}, bf16[352,768]{1,0:T(8,128)(2,1)S(1)}, u32[]{:S(2)}, u32[]{:S(2)}) collective-permute-start(bf16[352,768]{1,0:T(8,128)(2,1)S(1)} %pad_maximum_fusion.10), channel_id=1, source_target_pairs={{0,4},{4,0},{1,5},{5,1},{2,6},{6,2},{3,7},{7,3},{8,12},{12,8},{9,1... | collective-permute-start | bytes 1622024 | tf_op jit(solution)/shard_map/ppermute | solution.py:412
  255.3 44.4 %collective-permute-start.53 = (bf16[96,3072]{1,0:T(8,128)(2,1)S(1)}, bf16[96,3072]{1,0:T(8,128)(2,1)S(1)}, u32[]{:S(2)}, u32[]{:S(2)}) collective-permute-start(bf16[96,3072]{1,0:T(8,128)(2,1)S(1)} %pad_maximum_fusion.8), channel_id=1, source_target_pairs={{0,4},{4,0},{1,5},{5,1},{2,6},{6,2},{3,7},{7,3},{8,12},{12,8},{9,1... | collective-permute-start | bytes 1769480 | tf_op jit(solution)/shard_map/ppermute | solution.py:412
  (55 other events, 603.9 us)

commit v2 on v1

v2 whole, which is shorter than its diff:
```python
import jax
import jax.numpy as jnp
from jax import lax
from jax.experimental import pallas as pl
from jax.experimental.pallas import tpu as pltpu
from jax.sharding import Mesh
from jax.sharding import PartitionSpec as P

D = 768
HEADS = 12
HEAD_DIM = 64
PAIRS = HEADS // 2
ROWS = 256
OFFS = 512
TOKENS = 20480
GROUP = 4
PIECE = D // GROUP
HALF = PIECE // 2
WIDE = GROUP * D
REL_HALF = OFFS // GROUP // 2
REL_AT = 3 * HALF
FIRST = 3 * HALF + REL_HALF
OUT_AT = D // 2
NORM_AT = D // 2 + HALF
QUARTER = 128
SECOND = GROUP * QUARTER
SPAN = QUARTER + HALF
PART = ROWS // GROUP
X, Y, Z, CORE, LENGTH, SEQ = 0, 1, 2, 3, 4, 5
META = 16
EPSILON = 1e-07
MASKED = -1e30
SCALING = (3.0 * HEAD_DIM) ** (-0.5)
F32 = jnp.float32
LOW = jnp.bfloat16
MIB = 1024 * 1024


def mm(a, b):
    return lax.dot_general(a, b, (((1,), (0,)), ((), ())), preferred_element_type=F32)


def mm_nt(a, b):
    return lax.dot_general(a, b, (((1,), (1,)), ((), ())), preferred_element_type=F32)


def mm_tn(a, b):
    return lax.dot_general(a, b, (((0,), (0,)), ((), ())), preferred_element_type=F32)


def iota(shape, dim):
    return lax.broadcasted_iota(jnp.int32, shape, dim)


def whole(ref, start, size):
    piece = ref[:, :, start : start + size, :]
    return piece.reshape(GROUP * 2 * size, piece.shape[3])


def run_copies(copies):
    for copy in copies:
        copy.start()
    for copy in copies:
        copy.wait()


class Copies:
    def __init__(self, sem):
        self.sem, self.made = sem, []

    def add(self, source, target):
        self.made.append(pltpu.make_async_copy(source, target, self.sem.at[len(self.made)]))

    def start(self):
        for copy in self.made:
            copy.start()

    def wait(self):
        for copy in self.made:
            copy.wait()


def near_of(core):
    return 1 + 2 * core


def far_of(core):
    return 3 - 2 * core


def assist_of(meta_ref, core):
    return jnp.where(core == 0, meta_ref[Y], meta_ref[Z])


def position(distance, near):
    far = 4 - near
    place = jnp.where(distance == near, 1, jnp.where(distance == far, 2, 0))
    return jnp.where(distance == 0, 3, place)


def pack_body(
    coord_ref, length_ref, hidden_ref, grad_ref, own_q, own_k, own_v, own_rel, own_outer, own_out, own_inner, norm_ref,
    meta_ref, block_ref, *rest,
):
    rows_out, sem, tail_sem = rest
    first_ref, second_ref = block_ref.at[pl.ds(0, FIRST)], block_ref.at[pl.ds(FIRST, SPAN)]
    x, y, z, core = (coord_ref[i] for i in range(4))
    for i in range(4):
        meta_ref[i] = coord_ref[i]
    lengths = [length_ref[i] for i in range(GROUP)]
    dealing = []
    for i in range(GROUP):
        rank = jnp.int32(0)
        for j in range(GROUP):
            if j != i:
                ahead = lengths[j] >= lengths[i] if j < i else lengths[j] > lengths[i]
                rank = rank + ahead.astype(jnp.int32)
        dealing.append(rank)
    length = jnp.int32(0)
    for i in range(GROUP):
        length = length + jnp.where(dealing[i] == x, lengths[i], 0)
    meta_ref[LENGTH] = length
    copies = Copies(sem)
    for k in range(GROUP):
        source = jnp.int32(0)
        for i in range(GROUP):
            source = source + jnp.where(dealing[i] == (x ^ k), i, 0)
        meta_ref[SEQ + k] = source
        copies.add(hidden_ref.at[source], rows_out.at[x ^ k, 0])
        copies.add(grad_ref.at[source], rows_out.at[x ^ k, 1])
    for i in range(SEQ + GROUP, META):
        meta_ref[i] = jnp.int32(0)
    for i, ref in enumerate((own_q, own_k, own_v, own_rel)):
        size = REL_HALF if i == 3 else HALF
        copies.add(ref.at[pl.ds(core * size, size)], first_ref.at[pl.ds(i * HALF, size)])
    quarter = jnp.where(core == 0, y, z)
    copies.add(
        own_inner.at[pl.ds(core * HALF, HALF), pl.ds(pl.multiple_of(quarter * D, D), D)],
        second_ref.at[pl.ds(QUARTER, HALF)],
    )
    copies.start()
    tail = Copies(tail_sem)

    @pl.when(quarter < 3)
    def _():
        copy = pltpu.make_async_copy(
            own_outer.at[pl.ds(core * 3 * QUARTER + quarter * QUARTER, QUARTER)], second_ref.at[pl.ds(0, QUARTER)],
            tail_sem.at[0],
        )
        copy.start()
        copy.wait()

    @pl.when(quarter == 3)
    def _():
        tail.add(own_out.at[pl.ds(core * HALF, HALF)], second_ref.at[pl.ds(0, HALF)])
        tail.add(norm_ref, second_ref.at[pl.ds(HALF, QUARTER - HALF)])
        tail.start()
        tail.wait()

    copies.wait()


def pack(coords, lengths, hidden, grad_out, own_first, own_second, norm_block):
    shape = jax.ShapeDtypeStruct
    scalars, anywhere = pl.BlockSpec(memory_space=pltpu.SMEM), pl.BlockSpec(memory_space=pltpu.HBM)
    full = pl.BlockSpec(memory_space=pltpu.VMEM)
    return pl.pallas_call(
        pack_body,
        out_shape=(
            shape((META,), jnp.int32), shape((FIRST + SPAN, D), LOW), shape((GROUP, 2, PART, D), LOW),
        ),
        in_specs=[scalars, scalars] + [anywhere] * 10,
        out_specs=(scalars, full, full),
        scratch_shapes=[pltpu.SemaphoreType.DMA((13,)), pltpu.SemaphoreType.DMA((2,))],
        compiler_params=pltpu.CompilerParams(vmem_limit_bytes=60 * MIB),
        name="pack",
    )(coords, lengths, hidden, grad_out, *own_first, *own_second, norm_block)


def load_rows(copies, rows_ref, which, target):
    for member in range(GROUP):
        copies.add(rows_ref.at[member, which], target.at[pl.ds(member * PART, PART)])


def load_first(meta_ref, copies, own, pieces, w_ref):
    x, core = meta_ref[X], meta_ref[CORE]
    near, far = x ^ near_of(core), x ^ far_of(core)
    slots = ((near, core), (far, core), (x ^ 2, core), (far, 1 - core), (near, 1 - core), (x ^ 2, 1 - core))
    for piece, (slot, half) in zip(pieces, slots):
        copies.add(piece.at[pl.ds(0, FIRST)], w_ref.at[slot, half])
    for half in range(2):
        for i, ref in enumerate(own):
            size = REL_HALF if i == 3 else HALF
            copies.add(ref.at[pl.ds(half * size, size)], w_ref.at[x, half, pl.ds(i * HALF, size)])


def load_second(meta_ref, copies, own, pieces, w_ref, in_ref):
    own_outer, own_out, own_norm, own_inner = own
    x = meta_ref[X]
    for side in range(2):
        core = meta_ref[CORE] if side == 0 else 1 - meta_ref[CORE]
        assist = assist_of(meta_ref, core)
        arrived, (near, far, across_outer, across_inner) = pieces[7 * side : 7 * side + 3], pieces[7 * side + 3 : 7 * side + 7]
        for i, slot in enumerate((x ^ near_of(core), x ^ far_of(core), x ^ 2)):
            base = arrived[i]
            for outer, inner, quarter in (
                (base.at[pl.ds(FIRST, QUARTER)], base.at[pl.ds(FIRST + QUARTER, HALF)], assist),
                (near.at[i, pl.ds(0, QUARTER)], near.at[i, pl.ds(QUARTER, HALF)], assist ^ 1),
                (far.at[i, pl.ds(0, QUARTER)], far.at[i, pl.ds(QUARTER, HALF)], assist ^ 3),
                (across_outer.at[i], across_inner.at[i], assist ^ 2),
            ):
                copies.add(outer, w_ref.at[slot, core, pl.ds(quarter * QUARTER, QUARTER)])
                copies.add(
                    inner, in_ref.at[pl.ds(slot * PIECE + core * HALF, HALF), pl.ds(pl.multiple_of(quarter * D, D), D)]
                )
    for half in range(2):
        copies.add(own_outer.at[pl.ds(half * 3 * QUARTER, 3 * QUARTER)], w_ref.at[x, half, pl.ds(0, 3 * QUARTER)])
        copies.add(own_out.at[pl.ds(half * HALF, HALF)], w_ref.at[x, half, pl.ds(OUT_AT, HALF)])
    copies.add(own_norm, w_ref.at[x, 0, pl.ds(NORM_AT, QUARTER - HALF)])
    copies.add(own_inner, in_ref.at[pl.ds(x * PIECE, PIECE)])


def select_halves(meta_ref, value):
    half = value.shape[0] // 2
    low, high = value[:half].astype(LOW), value[half:].astype(LOW)
    first_core = meta_ref[CORE] == 0
    return jnp.where(first_core, low, high), jnp.where(first_core, high, low)


def heads_forward(meta_ref, first_pair, refs, probs_ref, ctx_ref):
    q_ref, k_ref, v_ref, pk_ref, pq_ref = refs
    length = meta_ref[LENGTH]
    valid = iota((ROWS, ROWS), 1) < length
    side = iota((ROWS, 2 * HEAD_DIM), 1) // HEAD_DIM

    def pair_step(pair, carry):
        out_cols = pl.ds(pl.multiple_of((pair - first_pair) * 2 * HEAD_DIM, 2 * HEAD_DIM), 2 * HEAD_DIM)
        cols = pl.ds(pl.multiple_of(pair * 2 * HEAD_DIM, 2 * HEAD_DIM), 2 * HEAD_DIM)
        q_pair, k_pair, v_pair = q_ref[:, cols], k_ref[:, cols], v_ref[:, cols]
        pk_pair, pq_pair = pk_ref[:, cols], pq_ref[:, cols]
        zero = jnp.zeros_like(q_pair)
        contexts = []
        for h in range(2):
            mine = side == h
            q_head = jnp.where(mine, q_pair, zero)
            k_head = jnp.where(mine, k_pair, zero)
            content = mm_nt(q_head, k_pair)
            to_off = mm_nt(q_head, pk_pair)
            from_off = mm_nt(k_head, pq_pair)
            to_rel = pltpu.roll(to_off, ROWS + 1, 1, stride=1, stride_axis=0)[:, :ROWS]
            from_rel = pltpu.roll(from_off, ROWS + 1, 1, stride=1, stride_axis=0)[:, :ROWS]
            scores = (content + to_rel + from_rel.T) * SCALING
            scores = jnp.where(valid, scores, MASKED)
            top = jnp.max(scores, axis=1, keepdims=True)
            shifted = jnp.exp(scores - top)
            summed = jnp.sum(shifted, axis=1, keepdims=True)
            probs = (shifted * (1.0 / summed)).astype(LOW)
            probs_ref[2 * (pair - first_pair) + h] = probs
            contexts.append(mm(probs, v_pair))
        ctx_ref[:, out_cols] = jnp.where(side == 0, contexts[0], contexts[1]).astype(LOW)
        return carry

    lax.fori_loop(first_pair, first_pair + PAIRS // 2, pair_step, 0)


def attend_forward_body(
    meta_ref, bucket_ref, rows_ref, own_q, own_k, own_v, own_rel, p0, p1, p2, p3, p4, p5,
    tok_ref, q_ref, k_ref, v_ref, pk_ref, pq_ref, relw_ref, probs_ref, ctx_ref,
    w_ref, sem,
):
    copies = Copies(sem)
    load_rows(copies, rows_ref, 0, tok_ref)
    load_first(meta_ref, copies, (own_q, own_k, own_v, own_rel), (p0, p1, p2, p3, p4, p5), w_ref)
    copies.start()
    copies.wait()
    tok = tok_ref[...]
    rel = whole(w_ref, REL_AT, REL_HALF)
    pick = (bucket_ref[...] == iota((OFFS, OFFS), 1)).astype(LOW)
    relw = mm(pick, rel).astype(LOW)
    relw_ref[...] = relw
    w_query = whole(w_ref, 0, HALF)
    q_ref[...] = mm(tok, w_query).astype(LOW)
    pq_ref[...] = mm(relw, w_query).astype(LOW)
    w_key = whole(w_ref, HALF, HALF)
    k_ref[...] = mm(tok, w_key).astype(LOW)
    pk_ref[...] = mm(relw, w_key).astype(LOW)
    v_ref[...] = mm(tok, whole(w_ref, 2 * HALF, HALF)).astype(LOW)
    heads_forward(meta_ref, 0, (q_ref, k_ref, v_ref, pk_ref, pq_ref), probs_ref, ctx_ref)


def attend_forward_two_body(meta_ref, q_ref, k_ref, v_ref, pk_ref, pq_ref, probs_ref, ctx_ref):
    heads_forward(meta_ref, PAIRS // 2, (q_ref, k_ref, v_ref, pk_ref, pq_ref), probs_ref, ctx_ref)


def attend_forward(meta, bucket_column, rows, own, pieces):
    shape = jax.ShapeDtypeStruct
    full, anywhere = pl.BlockSpec(memory_space=pltpu.VMEM), pl.BlockSpec(memory_space=pltpu.HBM)
    return pl.pallas_call(
        attend_forward_body,
        out_shape=(
            *(shape((ROWS, D), LOW),) * 4,
            shape((OFFS, D), LOW), shape((OFFS, D), LOW), shape((OFFS, D), LOW),
            shape((HEADS // 2, ROWS, ROWS), LOW), shape((ROWS, D // 2), LOW),
        ),
        in_specs=[pl.BlockSpec(memory_space=pltpu.SMEM), full] + [anywhere] * 11,
        out_specs=(full,) * 9,
        scratch_shapes=[pltpu.VMEM((GROUP, 2, FIRST, D), LOW), pltpu.SemaphoreType.DMA((18,))],
        compiler_params=pltpu.CompilerParams(vmem_limit_bytes=28 * MIB),
        cost_estimate=pl.CostEstimate(flops=12_000_000_000, bytes_accessed=40_000_000, transcendentals=800_000),
        name="attend_forward",
    )(meta, bucket_column, rows, *own, *pieces)


def attend_forward_two(meta, saved):
    shape = jax.ShapeDtypeStruct
    full = pl.BlockSpec(memory_space=pltpu.VMEM)
    return pl.pallas_call(
        attend_forward_two_body,
        out_shape=(shape((HEADS // 2, ROWS, ROWS), LOW), shape((ROWS, D // 2), LOW)),
        in_specs=[pl.BlockSpec(memory_space=pltpu.SMEM)] + [full] * 5,
        out_specs=(full,) * 2,
        compiler_params=pltpu.CompilerParams(vmem_limit_bytes=24 * MIB),
        cost_estimate=pl.CostEstimate(flops=8_000_000_000, bytes_accessed=20_000_000, transcendentals=400_000),
        name="attend_forward_two",
    )(meta, *saved)


def heads_back(first_pair, count, refs, outs):
    q_ref, k_ref, v_ref, pk_ref, pq_ref, probs_ref, gctx_ref = refs
    gq_ref, gk_ref, gv_ref, gpk_ref, gpq_ref, qr_ref, kr_ref = outs
    flip = (iota((ROWS, ROWS), 0) + iota((ROWS, ROWS), 1) == ROWS - 1).astype(LOW)
    qr_ref[...] = mm(flip, q_ref[...]).astype(LOW)
    kr_ref[...] = mm(flip, k_ref[...]).astype(LOW)
    side = iota((ROWS, 2 * HEAD_DIM), 1) // HEAD_DIM
    side_off = iota((OFFS, 2 * HEAD_DIM), 1) // HEAD_DIM
    blank = jnp.zeros((ROWS, OFFS - ROWS), F32)

    def pair_step(pair, carry):
        cols = pl.ds(pl.multiple_of(pair * 2 * HEAD_DIM, 2 * HEAD_DIM), 2 * HEAD_DIM)
        q_pair, k_pair, v_pair = q_ref[:, cols], k_ref[:, cols], v_ref[:, cols]
        pk_pair, pq_pair, gctx_pair = pk_ref[:, cols], pq_ref[:, cols], gctx_ref[:, cols]
        qr_pair, kr_pair = qr_ref[:, cols], kr_ref[:, cols]
        zero = jnp.zeros_like(q_pair)
        parts = []
        for h in range(2):
            gctx_head = jnp.where(side == h, gctx_pair, zero)
            grad_probs = mm_nt(gctx_head, v_pair)
            probs_low = probs_ref[2 * (pair - first_pair) + h]
            probs = probs_low.astype(F32)
            inner = jnp.sum(probs * grad_probs, axis=1, keepdims=True)
            grad_scores = (probs * (grad_probs - inner)).astype(LOW)
            g_value = mm_tn(probs_low, gctx_pair)
            rows_back = mm(flip, grad_scores)
            cols_back = mm_nt(flip, grad_scores)
            to_off = pltpu.roll(jnp.concatenate([rows_back, blank], axis=1), 0, 1, stride=1, stride_axis=0).astype(LOW)
            from_off = pltpu.roll(jnp.concatenate([cols_back, blank], axis=1), 0, 1, stride=1, stride_axis=0).astype(LOW)
            g_query = mm(rows_back.astype(LOW), k_pair) + mm(to_off, pk_pair)
            g_key = mm(cols_back.astype(LOW), q_pair) + mm(from_off, pq_pair)
            g_pk = mm_tn(to_off, qr_pair)
            g_pq = mm_tn(from_off, kr_pair)
            parts.append((g_value, g_query, g_key, g_pk, g_pq))
        first, second = parts
        gv_ref[:, cols] = jnp.where(side == 0, first[0], second[0]).astype(LOW)
        gq_ref[:, cols] = (jnp.where(side == 0, first[1], second[1]) * SCALING).astype(LOW)
        gk_ref[:, cols] = (jnp.where(side == 0, first[2], second[2]) * SCALING).astype(LOW)
        gpk_ref[:, cols] = (jnp.where(side_off == 0, first[3], second[3]) * SCALING).astype(LOW)
        gpq_ref[:, cols] = (jnp.where(side_off == 0, first[4], second[4]) * SCALING).astype(LOW)
        return carry

    lax.fori_loop(first_pair, first_pair + count, pair_step, 0)
    return flip


def attend_back_one_body(
    q_ref, k_ref, v_ref, pk_ref, pq_ref, probs_ref, gctx_ref,
    gq_ref, gk_ref, gv_ref, gpk_ref, gpq_ref, qr_ref, kr_ref,
):
    heads_back(
        0, PAIRS // 2, (q_ref, k_ref, v_ref, pk_ref, pq_ref, probs_ref, gctx_ref),
        (gq_ref, gk_ref, gv_ref, gpk_ref, gpq_ref, qr_ref, kr_ref),
    )


def attend_back_two_body(
    meta_ref, q_ref, k_ref, v_ref, pk_ref, pq_ref, probs_ref, gctx_ref, hq, hk, hv, hpk, hpq,
    tok_ref, relw_ref, gres_ref, bucket_ref,
    own_q, own_k, own_v, own_rel, p0, p1, p2, p3, p4, p5,
    out_ref,
    home_ref, keep_ref, send_ref,
    gq_ref, gk_ref, gv_ref, gpk_ref, gpq_ref, qr_ref, kr_ref, gtok_ref, w_ref, sem,
):
    copies = Copies(sem)
    load_first(meta_ref, copies, (own_q, own_k, own_v, own_rel), (p0, p1, p2, p3, p4, p5), w_ref)
    copies.start()
    for target, done in ((gq_ref, hq), (gk_ref, hk), (gv_ref, hv), (gpk_ref, hpk), (gpq_ref, hpq)):
        target[:, : D // 2] = done[...]
    flip = heads_back(
        PAIRS // 2, PAIRS // 2, (q_ref, k_ref, v_ref, pk_ref, pq_ref, probs_ref, gctx_ref),
        (gq_ref, gk_ref, gv_ref, gpk_ref, gpq_ref, qr_ref, kr_ref),
    )
    copies.wait()
    tok, relw = tok_ref[...], relw_ref[...]
    g_query = mm(flip, gq_ref[...]).astype(LOW)
    w_query = whole(w_ref, 0, HALF)
    g_tok = gres_ref[...] + mm_nt(g_query, w_query)
    g_rel = mm_nt(gpq_ref[...], w_query)

    x, core = meta_ref[X], meta_ref[CORE]

    def put(start, size, value):
        for shard in range(GROUP):
            keep, send = select_halves(meta_ref, value[shard * 2 * size : (shard + 1) * 2 * size])
            keep_ref[position(x ^ shard, near_of(core)), start : start + size] = keep
            send_ref[position(x ^ shard, far_of(core)), start : start + size] = send

    put(0, HALF, mm_tn(tok, g_query) + mm_tn(relw, gpq_ref[...]))
    g_key = mm(flip, gk_ref[...]).astype(LOW)
    w_key = whole(w_ref, HALF, HALF)
    g_tok = g_tok + mm_nt(g_key, w_key)
    g_rel = (g_rel + mm_nt(gpk_ref[...], w_key)).astype(LOW)
    put(HALF, HALF, mm_tn(tok, g_key) + mm_tn(relw, gpk_ref[...]))
    g_value = gv_ref[...]
    gtok_ref[...] = (g_tok + mm_nt(g_value, whole(w_ref, 2 * HALF, HALF))).astype(LOW)
    put(2 * HALF, HALF, mm_tn(tok, g_value))
    pick = (bucket_ref[...] == iota((OFFS, OFFS), 1)).astype(LOW)
    put(REL_AT, REL_HALF, mm_tn(pick, g_rel))
    for member in range(GROUP):
        home_ref[member, 0] = out_ref[member * PART : (member + 1) * PART, :]
        home_ref[member, 1] = gtok_ref[member * PART : (member + 1) * PART, :]


def attend_back_one(saved, gctx):
    shape = jax.ShapeDtypeStruct
    full = pl.BlockSpec(memory_space=pltpu.VMEM)
    return pl.pallas_call(
        attend_back_one_body,
        out_shape=(*(shape((ROWS, D // 2), LOW),) * 3, *(shape((OFFS, D // 2), LOW),) * 2),
        in_specs=[full] * 7,
        out_specs=(full,) * 5,
        scratch_shapes=[pltpu.VMEM((ROWS, D), LOW), pltpu.VMEM((ROWS, D), LOW)],
        compiler_params=pltpu.CompilerParams(vmem_limit_bytes=24 * MIB),
        cost_estimate=pl.CostEstimate(flops=8_000_000_000, bytes_accessed=20_000_000, transcendentals=0),
        name="attend_back_one",
    )(*saved, gctx)


def attend_back_two(meta, saved, gctx, half_done, tok, relw, gres, bucket_column, own, pieces, out):
    shape = jax.ShapeDtypeStruct
    full, anywhere = pl.BlockSpec(memory_space=pltpu.VMEM), pl.BlockSpec(memory_space=pltpu.HBM)
    return pl.pallas_call(
        attend_back_two_body,
        out_shape=(shape((GROUP, 2, PART, D), LOW), shape((GROUP, FIRST, D), LOW), shape((GROUP, FIRST, D), LOW)),
        in_specs=[pl.BlockSpec(memory_space=pltpu.SMEM)] + [full] * 16 + [anywhere] * 10 + [full],
        out_specs=(full,) * 3,
        scratch_shapes=[
            *(pltpu.VMEM((ROWS, D), LOW),) * 3, *(pltpu.VMEM((OFFS, D), LOW),) * 2, *(pltpu.VMEM((ROWS, D), LOW),) * 3,
            pltpu.VMEM((GROUP, 2, FIRST, D), LOW), pltpu.SemaphoreType.DMA((14,)),
        ],
        compiler_params=pltpu.CompilerParams(vmem_limit_bytes=36 * MIB),
        cost_estimate=pl.CostEstimate(flops=14_000_000_000, bytes_accessed=40_000_000, transcendentals=0),
        name="attend_back_two",
    )(meta, *saved, gctx, *half_done, tok, relw, gres, bucket_column, *own, *pieces, out)


def feed_body(
    meta_ref, tok_ref, ctx_one_ref, ctx_two_ref, rows_ref, own_outer, own_out, own_norm, own_inner, *rest,
):
    pieces, rest = rest[:14], rest[14:]
    out_ref, gctx_ref, gres_ref, keep_ref, send_ref, keep_in_ref, send_in_ref = rest[:7]
    up_ref, low_ref, act_ref, slope_ref, w_ref, in_ref, sem = rest[7:]
    copies = Copies(sem)
    load_rows(copies, rows_ref, 1, up_ref)
    load_second(meta_ref, copies, (own_outer, own_out, own_norm, own_inner), pieces, w_ref, in_ref)
    copies.start()
    copies.wait()
    x, core = meta_ref[X], meta_ref[CORE]
    assist, assist_peer = assist_of(meta_ref, core), assist_of(meta_ref, 1 - core)

    def put_outer(shard, quarter, keep, send, start):
        rows = slice(start, start + keep.shape[0])
        keep_ref[position(assist ^ quarter, 1), position(x ^ shard, near_of(core)), rows] = keep
        send_ref[position(assist_peer ^ quarter, 1), position(x ^ shard, far_of(core)), rows] = send

    def put_inner(shard, quarter, keep, send):
        keep_in_ref[position(assist ^ quarter, 3), position(x ^ shard, near_of(core))] = keep
        send_in_ref[position(assist_peer ^ quarter, 3), position(x ^ shard, far_of(core))] = send

    length = meta_ref[LENGTH]
    mask = (iota((ROWS, 1), 0) < length).astype(F32)
    norm_rows = [w_ref[s, 0, NORM_AT : NORM_AT + QUARTER - HALF, :].astype(F32)[:1] for s in range(GROUP)]
    gain_one, bias_one, gain_two, bias_two = (
        jnp.concatenate([row[:, i * PIECE : (i + 1) * PIECE] for row in norm_rows], axis=1) for i in range(4)
    )
    token = tok_ref[...].astype(F32)
    ctx = jnp.concatenate([ctx_one_ref[...], ctx_two_ref[...]], axis=1)
    w_out = whole(w_ref, OUT_AT, HALF)
    attn = mm(ctx, w_out)

    def norm(values):
        center = values - jnp.mean(values, axis=1, keepdims=True)
        inverse = lax.rsqrt(jnp.mean(center * center, axis=1, keepdims=True) + EPSILON)
        return center * inverse, inverse

    def norm_back(upstream, normed, inverse, gain):
        scaled = upstream * gain
        plain = jnp.mean(scaled, axis=1, keepdims=True)
        cross = jnp.mean(scaled * normed, axis=1, keepdims=True)
        return inverse * (scaled - plain - normed * cross)

    def total(values):
        return jnp.sum(values, axis=0, keepdims=True)

    normed_one, inverse_one = norm(token + attn)
    hidden_one = normed_one * gain_one + bias_one
    low_ref[...] = hidden_one.astype(LOW)

    def columns(c):
        return pl.ds(pl.multiple_of(c * D, D), D)

    def outer_rows(c):
        return w_ref[c, :, 0 : D // 2, :].reshape(D, D)

    def forward_step(c, ffn):
        inner = mm(low_ref[...], in_ref[:, columns(c)])
        cumulative = 0.5 * (1.0 + lax.erf(inner * 0.5**0.5))
        density = jnp.exp(-0.5 * inner * inner) * 0.3989422804014327
        act = (inner * cumulative).astype(LOW)
        act_ref[c] = act
        slope_ref[c] = cumulative + inner * density
        return ffn + mm(act, outer_rows(c))

    ffn = lax.fori_loop(0, GROUP, forward_step, jnp.zeros((ROWS, D), F32))
    normed_two, inverse_two = norm(hidden_one + ffn)
    layer = (normed_two * gain_two + bias_two) * mask
    out_ref[...] = layer.astype(LOW)
    squares = [token * token * mask, attn * attn * mask, ffn * ffn * mask, layer * layer]
    sums = [jnp.sum(total(s), axis=1, keepdims=True) for s in squares]
    grad_y = up_ref[...].astype(F32) * mask
    grad_gain_two = total(grad_y * normed_two)
    grad_bias_two = total(grad_y)
    grad_two = norm_back(grad_y, normed_two, inverse_two, gain_two)
    grad_ffn = grad_two.astype(LOW)

    def back_step(c, grad_hidden):
        grad_act = mm_nt(grad_ffn, outer_rows(c))
        grad_inner = (grad_act * slope_ref[c]).astype(LOW)
        keep, send = select_halves(meta_ref, mm_tn(act_ref[c], grad_ffn))
        for quarter in range(3):
            rows = slice(quarter * QUARTER, (quarter + 1) * QUARTER)
            put_outer(c, quarter, keep[rows], send[rows], 0)
        grad_w = mm_tn(low_ref[...], grad_inner)
        for s in range(GROUP):
            put_inner(s, c, *select_halves(meta_ref, grad_w[s * PIECE : (s + 1) * PIECE]))
        return grad_hidden + mm_nt(grad_inner, in_ref[:, columns(c)])

    grad_hidden = lax.fori_loop(0, GROUP, back_step, grad_two)
    grad_gain_one = total(grad_hidden * normed_one)
    grad_bias_one = total(grad_hidden)
    grad_one = norm_back(grad_hidden, normed_one, inverse_one, gain_one)
    gres_ref[...] = grad_one
    grad_attn = grad_one.astype(LOW)
    grad_out = mm_tn(ctx, grad_attn)
    for s in range(GROUP):
        put_outer(s, 3, *select_halves(meta_ref, grad_out[s * PIECE : (s + 1) * PIECE]), 0)
    gctx_ref[...] = mm_nt(grad_attn, w_out).astype(LOW)
    lane = iota((1, D), 1)
    stats = jnp.zeros((1, D), F32)
    for i, value in enumerate(sums):
        stats = jnp.where(lane == i, value, stats)
    low = stats - stats.astype(LOW).astype(F32)
    zeros = jnp.zeros((1, D), F32)
    norm_rows = (grad_gain_one, grad_bias_one, grad_gain_two, grad_bias_two)
    for s in range(GROUP):
        row = jnp.concatenate([r[:, s * PIECE : (s + 1) * PIECE] for r in norm_rows], axis=1)
        block = jnp.concatenate([row] + [zeros] * 31 + [stats, low] + [zeros] * 30, axis=0)
        put_outer(s, 3, *select_halves(meta_ref, block), HALF)


def feed(meta, tok, ctx_one, ctx_two, rows, own, pieces):
    shape = jax.ShapeDtypeStruct
    full, anywhere = pl.BlockSpec(memory_space=pltpu.VMEM), pl.BlockSpec(memory_space=pltpu.HBM)
    block, wide = shape((GROUP, GROUP, QUARTER, D), LOW), shape((GROUP, GROUP, HALF, D), LOW)
    return pl.pallas_call(
        feed_body,
        out_shape=(
            shape((ROWS, D), LOW), shape((ROWS, D), LOW), shape((ROWS, D), F32), block, block, wide, wide
        ),
        in_specs=[pl.BlockSpec(memory_space=pltpu.SMEM)] + [full] * 3 + [anywhere] * 19,
        out_specs=(full,) * 7,
        scratch_shapes=[
            *(pltpu.VMEM((ROWS, D), LOW),) * 2, pltpu.VMEM((GROUP, ROWS, D), LOW), pltpu.VMEM((GROUP, ROWS, D), F32),
            pltpu.VMEM((GROUP, 2, SECOND, D), LOW), pltpu.VMEM((D, WIDE), LOW), pltpu.SemaphoreType.DMA((58,)),
        ],
        compiler_params=pltpu.CompilerParams(vmem_limit_bytes=48 * MIB),
        cost_estimate=pl.CostEstimate(flops=16_000_000_000, bytes_accessed=60_000_000, transcendentals=1_600_000),
        name="feed",
    )(meta, tok, ctx_one, ctx_two, rows, *own, *pieces)


def finish_body(
    meta_ref, mine, other, rows_ref,
    q_ref, k_ref, v_ref, rel_ref, outer_ref, wout_ref, inner_ref, extra_ref, out_ref, gtok_ref,
):
    for piece, side in ((mine, 0), (other, 1)):
        core = meta_ref[CORE] if side == 0 else 1 - meta_ref[CORE]
        assist = assist_of(meta_ref, core)
        for i, ref in enumerate((q_ref, k_ref, v_ref, rel_ref)):
            size = REL_HALF if i == 3 else HALF
            ref[pl.ds(pl.multiple_of(core * size, size), size), :] = piece[i * HALF : i * HALF + size, :].astype(F32)
        for distance in range(GROUP):
            quarter = assist ^ distance
            at = FIRST + distance * SPAN
            block = piece[at : at + QUARTER, :].astype(F32)

            @pl.when(quarter < 3)
            def _():
                outer_ref[pl.ds(pl.multiple_of(core * 3 * QUARTER + quarter * QUARTER, QUARTER), QUARTER), :] = block

            @pl.when(quarter == 3)
            def _():
                wout_ref[pl.ds(pl.multiple_of(core * HALF, HALF), HALF), :] = block[:HALF]
                extra_ref[core] = block[HALF:]

            inner_ref[
                pl.ds(pl.multiple_of(core * HALF, HALF), HALF), pl.ds(pl.multiple_of(quarter * D, D), D)
            ] = piece[at + QUARTER : at + SPAN, :].astype(F32)
    for k in range(GROUP):
        member = meta_ref[X] ^ k
        out_ref[meta_ref[SEQ + k]] = rows_ref[member, 0]
        gtok_ref[meta_ref[SEQ + k]] = rows_ref[member, 1]


def finish(meta, mine, other, rows):
    shape = jax.ShapeDtypeStruct
    full = pl.BlockSpec(memory_space=pltpu.VMEM)
    return pl.pallas_call(
        finish_body,
        out_shape=(
            *(shape((PIECE, D), F32),) * 3, shape((OFFS // GROUP, D), F32),
            shape((D, D), F32), shape((PIECE, D), F32), shape((PIECE, WIDE), F32), shape((2, QUARTER - HALF, D), F32),
            *(shape((GROUP, PART, D), LOW),) * 2,
        ),
        in_specs=[pl.BlockSpec(memory_space=pltpu.SMEM)] + [full] * 3,
        out_specs=(full,) * 10,
        compiler_params=pltpu.CompilerParams(vmem_limit_bytes=24 * MIB),
        name="finish",
    )(meta, mine, other, rows)


NEAR, FAR = (1, 3), (3, 1)


def hop_x(value, flips):
    pairs = [(c * 4 + i, c * 4 + (i ^ flips[c])) for c in range(2) for i in range(4)]
    return lax.ppermute(value, ("core", "shard"), pairs)


def hop_yz(value, flip, swapped=False):
    pairs = []
    for y in range(4):
        for z in range(4):
            for c in range(2):
                along_y = (c == 0) != swapped
                ty, tz = (y ^ flip, z) if along_y else (y, z ^ flip)
                pairs.append(((y * 4 + z) * 2 + c, (ty * 4 + tz) * 2 + c))
    return lax.ppermute(value, ("y", "z", "core"), pairs)


def swap(value):
    return lax.ppermute(value, "core", [(0, 1), (1, 0)])


def after(value, *others):
    return lax.optimization_barrier((value, *others))[0]


def add(*values):
    total = values[0].astype(F32)
    for value in values[1:]:
        total = total + value.astype(F32)
    return total.astype(LOW)


def exchange_rows(rows):
    return lax.all_to_all(rows, "shard", split_axis=0, concat_axis=0, tiled=True)


def shards(
    hidden, grad_out, lengths, bucket, w_query, w_key, w_value, w_out, w_inner, w_outer, rel_table,
    ln1_gain, ln1_bias, ln2_gain, ln2_bias,
):
    coords = jnp.stack([lax.axis_index(name) for name in ("shard", "y", "z", "core")]).astype(jnp.int32)
    norm_block = jnp.concatenate(
        [jnp.concatenate([ln1_gain, ln1_bias, ln2_gain, ln2_bias])[None], jnp.zeros((31, D), LOW)], axis=0
    )
    bucket_column = jnp.concatenate([bucket[::-1], jnp.full((1,), -1, jnp.int32)])[:, None]
    own_first = (w_query, w_key, w_value, rel_table)
    meta, block, rows = pack(
        coords, lengths, hidden, grad_out, own_first, (w_outer, w_out, w_inner), norm_block
    )
    near, far = hop_x(block, NEAR), hop_x(block, FAR)
    rows = exchange_rows(rows)
    across = hop_x(near, FAR)
    swapped_near, swapped_far = swap(near), swap(far)
    base = jnp.stack([piece[FIRST:] for piece in (near, far, across)])
    base_near, base_far = hop_yz(base, 1), hop_yz(base, 3)
    pieces = (near, far, across, swapped_near, swapped_far, swap(across))
    tok, *saved, relw, probs, ctx = attend_forward(meta, bucket_column, rows, own_first, pieces)
    base_near, base_far, _ = lax.optimization_barrier((base_near, base_far, ctx))
    across_outer = hop_yz(base_near[:, :QUARTER], 3)
    across_inner = hop_yz(base_far[:, QUARTER:], 1)
    swapped = swap(base_near), swap(base_far)
    probs_two, ctx_two = attend_forward_two(meta, saved)
    swapped, across_outer, across_inner, _ = lax.optimization_barrier((swapped, across_outer, across_inner, ctx_two))
    arrived = (
        *pieces[:3], base_near, base_far, across_outer, across_inner,
        *pieces[3:], *swapped, swap(across_outer), swap(across_inner),
    )
    out, gctx, gres, keep, send, keep_in, send_in = feed(
        meta, tok, ctx, ctx_two, rows, (w_outer, w_out, norm_block, w_inner), arrived
    )
    other, other_in = swap(send), swap(send_in)
    half_done = attend_back_one((*saved, probs), gctx)
    leave = add(keep[:2], other[:2])
    leave_in = add(keep_in[:2], other_in[:2])
    came, came_in = hop_yz(leave, 1), hop_yz(leave_in, 3)
    half_done = after(tuple(half_done), leave, leave_in)
    leaving, keep_one, send_one = attend_back_two(
        meta, (*saved, probs_two), gctx, half_done, tok, relw, gres, bucket_column, own_first, pieces, out
    )
    other_one = swap(after(send_one, came, came_in))
    last = hop_yz(add(keep[2], other[2], came[0]), 3)
    last_in = hop_yz(add(keep_in[2], other_in[2], came_in[0]), 1)
    leave_one = add(keep_one[:2], other_one[:2])
    came_one = hop_x(leave_one, NEAR)
    came_one = after(came_one, last, last_in)
    leave_two = add(keep_one[2], other_one[2], came_one[0])
    last_one = hop_x(leave_two, FAR)
    last, last_in, _ = lax.optimization_barrier((last, last_in, leave_two))
    mine = add(keep[3], other[3], came[1], last)
    mine_in = add(keep_in[3], other_in[3], came_in[1], last_in)
    both = jnp.concatenate([mine, mine_in], axis=1)
    came_x = hop_x(both[:2], NEAR)
    home = exchange_rows(leaving)
    last_one = after(last_one, came_x)
    mine_one = add(keep_one[3], other_one[3], came_one[1], last_one)
    come_one = hop_yz(mine_one, 1, swapped=True)
    last_x = hop_x(after(add(both[2], came_x[0]), mine_one), FAR)
    mine_one = add(mine_one, after(come_one, last_x))
    come_one = hop_yz(mine_one, 3, swapped=True)
    both = after(add(both[3], came_x[1], last_x), mine_one)
    step = hop_yz(both, 1, swapped=True)
    mine_one = add(mine_one, after(come_one, step))
    come_one = hop_yz(mine_one, 1)
    both = after(add(both, step), mine_one)
    step = hop_yz(both, 3, swapped=True)
    mine_one = add(mine_one, after(come_one, step))
    come_one = hop_yz(mine_one, 3)
    both = after(add(both, step), mine_one)
    both = [both, *(hop_yz(both, flip) for flip in (1, 3, 2))]
    both[1], both[2], both[3] = both[1], both[3], both[2]
    mine_one = add(mine_one, come_one)
    packed = after(jnp.concatenate([mine_one, *both], axis=0), home)
    q_grad, k_grad, v_grad, rel_grad, outer_grad, out_grad, inner_grad, extra, layer_output, grad_hidden = finish(
        meta, packed, swap(packed), home
    )
    norm_sums = extra[0, 0].reshape(GROUP, PIECE)
    stats = extra[1, 0, :GROUP] + extra[1, 1, :GROUP]
    return (
        layer_output, grad_hidden, q_grad, k_grad, v_grad, out_grad, inner_grad, outer_grad, rel_grad,
        norm_sums[0], norm_sums[1], norm_sums[2], norm_sums[3],
        jnp.sqrt(stats / (TOKENS * D)),
    )


def solution(mesh):
    split = Mesh(mesh.devices.reshape(4, 4, 2, 4), ("y", "z", "core", "shard"))
    rep = ("y", "z", "core")
    rows, vector = P("shard", None), P("shard")
    batch = P(rep, "shard", None)
    return jax.shard_map(
        shards,
        mesh=split,
        in_specs=(batch, batch, P(rep), P(), *(rows,) * 7, *(vector,) * 4),
        out_specs=(batch, batch, *(rows,) * 7, *(vector,) * 4, P()),
        check_vma=False,
    )
```

time: 312 us -> 241 us (0.77)
  other arithmetic: 37.5 us -> 9.73 us
  local copies, waits for them, and re-layouts: 26.6 us -> 7.14 us
  starting transfers between devices: 78.4 us -> 62.3 us
  waiting for transfers between devices: 104 us -> 88.5 us
  Pallas kernels: 58.1 us -> 68.4 us
    ppermute x39 -> x24, waiting for transfers between devices: 101 us -> 76.8 us  [the longest x7 43.2 us: hop_x(): return lax.ppermute(value, ('core', 'shard'), pairs)]
    convert_element_type x30 -> x16, other arithmetic: 18.2 us -> 5.43 us  [add(): return total.astype(LOW)]
    ppermute x15 -> x11, waiting for transfers between devices: 0.09 us -> 11.8 us  [swap(): return lax.ppermute(value, 'core', [(0, 1), (1, 0)])]
    concatenate x13 -> x1, other arithmetic: 10.3 us -> 0.05 us  [shards(): both = jnp.concatenate([mine, mine_in], axis=1)]
    pallas_call x2 -> x6, Pallas kernels: 35.8 us -> 45.3 us  [the longest x1 15.1 us: attend_back_two(): pl.pallas_call(attend_back_two_body, out_shape=(shape((GROUP, 2, PART, D)...]
    ppermute x39 -> x24, starting transfers between devices: 43.8 us -> 34.8 us  [the longest x17 25.7 us: hop_yz(): return lax.ppermute(value, ('y', 'z', 'core'), pairs)]
    ppermute x15 -> x11, starting transfers between devices: 26.5 us -> 18.8 us  [swap(): return lax.ppermute(value, 'core', [(0, 1), (1, 0)])]
    unnamed x52 -> x39, local copies, waits for them, and re-layouts: 8.75 us -> 1.44 us
  transfers between devices with their start and end apart: 56 -> 37, of which waited for: 22 -> 21; matrix products, arithmetic and copies ran while one was open for 18% -> 4% of each run, Pallas kernels for 5% -> 16%
where the time goes in v2:
time: 241 us; the launch traced here: 237 us
  waiting for transfers between devices  88.5 us (37%)
  Pallas kernels  68.4 us (28%)
  starting transfers between devices  62.3 us (26%)
  other arithmetic  9.73 us (4%)
  local copies, waits for them, and re-layouts  7.14 us (3%)
    ppermute x7, waiting for transfers between devices, hop_x(): return lax.ppermute(value, ('core', 'shard'), pairs)  43.2 us
    ppermute x17, waiting for transfers between devices, hop_yz(): return lax.ppermute(value, ('y', 'z', 'core'), pairs)  33.6 us
    ppermute x17, starting transfers between devices, hop_yz(): return lax.ppermute(value, ('y', 'z', 'core'), pairs)  25.7 us
    pallas_call x1, Pallas kernels, feed(): pl.pallas_call(feed_body, out_shape=(shape((ROWS, D), LOW), shape((ROWS,...  23.1 us
    ppermute x11, starting transfers between devices, swap(): return lax.ppermute(value, 'core', [(0, 1), (1, 0)])  18.8 us
    pallas_call x1, Pallas kernels, attend_back_two(): pl.pallas_call(attend_back_two_body, out_shape=(shape((GROUP, 2, PART, D)...  15.1 us
    ppermute x11, waiting for transfers between devices, swap(): return lax.ppermute(value, 'core', [(0, 1), (1, 0)])  11.8 us
    pallas_call x1, Pallas kernels, attend_forward(): pl.pallas_call(attend_forward_body, out_shape=(*(shape((ROWS, D), LOW),)...  10.8 us
  transfers between devices with their start and end apart: 37, of which 21 were waited for; matrix products, arithmetic and copies ran while one was open for 4% of the time, Pallas kernels for 16%

profile of v2, /device:TPU:17, one launch (start us, length us, event | category | flops | bytes accessed | tf_op | source)
XLA Modules:
  0.0 237.2 jit_solution(3009432881266521675)
XLA Ops:
  2.7 3.5 %pack.1 = (s32[16]{0:T(128)}, bf16[576,768]{1,0:T(8,128)(2,1)}, bf16[4,2,64,768]{3,2,1,0:T(8,128)(2,1)}) custom-call(s32[4]{0:T(128)} %pad_add_fusion.1.coord_ref, s32[4]{0:T(128)} %length_ref.1, bf16[4,64,768]{2,1,0:T(8,128)(2,1)} %hidden_ref.1, bf16[4,64,768]{2,1,0:T(8,128)(2,1)} %grad_ref.1, bf16[192,768]{1,0:T(8,128)(2,1)} %own_q.5, ...), custom_call_target="tpu_custom_call" | custom-call | tf_op jit(solution)/shard_map/pack/pallas_call | solution.py:167
  8.8 18.0 %collective-permute-done.p0.rest_0_ = bf16[576,768]{1,0:T(8,128)(2,1)S(1)} collective-permute-done((bf16[576,768]{1,0:T(8,128)(2,1)}, bf16[576,768]{1,0:T(8,128)(2,1)S(1)}, u32[]{:S(2)}, u32[]{:S(2)}) %collective-permute-start) | collective-permute-done | bytes 884768 | tf_op jit(solution)/shard_map/ppermute | solution.py:655
  27.6 4.8 %all-to-all-start = ((bf16[4,2,64,768]{3,2,1,0:T(8,128)(2,1)}), bf16[4,2,64,768]{3,2,1,0:T(8,128)(2,1)S(1)}, u32[]{:S(2)}, u32[]{:S(2)}) async-start(bf16[4,2,64,768]{3,2,1,0:T(8,128)(2,1)} %get-tuple-element.78), calls=%async_computation | async-start | bytes 1572864 | tf_op jit(solution)/shard_map/all_to_all | solution.py:685
  35.3 4.3 %collective-permute-done.2.p2.rest_2_ = bf16[576,768]{1,0:T(8,128)(2,1)} collective-permute-done((bf16[576,768]{1,0:T(8,128)(2,1)S(1)}, bf16[576,768]{1,0:T(8,128)(2,1)}, u32[]{:S(2)}, u32[]{:S(2)}) %collective-permute-start.2) | collective-permute-done | bytes 884768 | tf_op jit(solution)/shard_map/ppermute | solution.py:655
  39.6 8.8 %collective-permute-start.5 = (bf16[576,768]{1,0:T(8,128)(2,1)}, bf16[576,768]{1,0:T(8,128)(2,1)}, u32[]{:S(2)}, u32[]{:S(2)}) collective-permute-start(bf16[576,768]{1,0:T(8,128)(2,1)} %collective-permute-done.2.p2.rest_2_), channel_id=1, source_target_pairs={{0,4},{4,0},{1,5},{5,1},{2,6},{6,2},{3,7},{7,3},{8,12},{12,8},{9,1... | collective-permute-start | bytes 2654216 | tf_op jit(solution)/shard_map/ppermute | solution.py:670
  55.8 10.8 %attend_forward.1 = (bf16[256,768]{1,0:T(8,128)(2,1)S(1)}, bf16[256,768]{1,0:T(8,128)(2,1)S(1)}, bf16[256,768]{1,0:T(8,128)(2,1)S(1)}, bf16[256,768]{1,0:T(8,128...) custom-call(s32[16]{0:T(128)S(1)} %copy-done.8, ...), custom_call_target="tpu_custom_call" | custom-call | flops 12000000000 | bytes 40000000 | tf_op jit(solution)/shard_map/attend_forward/pallas_call | solution.py:298
  71.2 2.9 %collective-permute-start.10 = (bf16[3,128,768]{2,1,0:T(8,128)(2,1)S(1)}, bf16[3,128,768]{2,1,0:T(8,128)(2,1)S(1)}, u32[]{:S(2)}, u32[]{:S(2)}) collective-permute-start(bf16[3,128,768]{2,1,0:T(8,128)(2,1)S(1)} %slice.132), channel_id=1, source_target_pairs={{0,96},{4,28},{8,104},{12,20},{16,112},{20,12},{24,120},{28,4},{32... | collective-permute-start | bytes 1769480 | tf_op jit(solution)/shard_map/ppermute | solution.py:666
  74.1 5.5 %attend_forward_two.1 = (bf16[6,256,256]{2,1,0:T(8,128)(2,1)S(1)}, bf16[256,384]{1,0:T(8,128)(2,1)S(1)}) custom-call(s32[16]{0:T(128)S(1)} %copy-done.8, bf16[256,768]{1,0:T(8,128)(2,1)S(1)} %get-tuple-element.80.q_ref, bf16[256,768]{1,0:T(8,128)(2,1)S(1)} %get-tuple-element.81.k_ref, bf16[256,768]{1,0:T(8,128)(2,1)S(1)} %get-tuple-element.82.v_ref, ...), custom_call_target="tpu_custom_call" | custom-call | flops 8000000000 | bytes 20000000 | tf_op jit(solution)/shard_map/attend_forward_two/pallas_call | solution.py:317
  84.1 23.1 %feed.1 = (bf16[256,768]{1,0:T(8,128)(2,1)S(1)}, bf16[256,768]{1,0:T(8,128)(2,1)S(1)}, f32[256,768]{1,0:T(8,128)S(1)}, bf16[4,4,128,768]{3,2,1,0:T(8,128)(2,1)},...) custom-call(s32[16]{0:T(128)S(1)} %copy-done.8, ...), custom_call_target="tpu_custom_call" | custom-call | flops 16000000000 | bytes 60000000 | tf_op jit(solution)/shard_map/feed/pallas_call | solution.py:583
  107.8 6.0 %attend_back_one.1 = (bf16[256,384]{1,0:T(8,128)(2,1)S(1)}, bf16[256,384]{1,0:T(8,128)(2,1)S(1)}, bf16[256,384]{1,0:T(8,128)(2,1)S(1)}, bf16[512,384]{1,0:T(8,128)(2,1)S(1)}, bf16[512,384]{1,0:T(8,128)(2,1)S(1)}) custom-call(bf16[256,768]{1,0:T(8,128)(2,1)S(1)} %get-tuple-element.80.q_ref, bf16[256,768]{1,0:T(8,128)(2,1)S(1)} %get-tuple-element.81.k_ref, ...), custom_call_target="tpu_custom_call" | custom-call | flops 8000000000 | bytes 20000000 | tf_op jit(solution)/shard_map/attend_back_one/pallas_call | solution.py:435
  120.7 15.1 %attend_back_two.1 = (bf16[4,2,64,768]{3,2,1,0:T(8,128)(2,1)}, bf16[4,352,768]{2,1,0:T(8,128)(2,1)S(1)}, bf16[4,352,768]{2,1,0:T(8,128)(2,1)}) custom-call(s32[16]{0:T(128)S(1)} %copy-done.8, bf16[256,768]{1,0:T(8,128)(2,1)S(1)} %get-tuple-element.80.q_ref, bf16[256,768]{1,0:T(8,128)(2,1)S(1)} %get-tuple-element.81.k_ref, ...), custom_call_target="tpu_custom_call" | custom-call | flops 14000000000 | bytes 40000000 | tf_op jit(solution)/shard_map/attend_back_two/pallas_call | solution.py:450
  135.9 4.5 %collective-permute-done.18 = bf16[4,352,768]{2,1,0:T(8,128)(2,1)S(1)} collective-permute-done((bf16[4,352,768]{2,1,0:T(8,128)(2,1)}, bf16[4,352,768]{2,1,0:T(8,128)(2,1)S(1)}, u32[]{:S(2)}, u32[]{:S(2)}) %collective-permute-start.18) | collective-permute-done | bytes 2162720 | tf_op jit(solution)/shard_map/ppermute | solution.py:670
  140.6 3.6 %collective-permute-start.19 = (bf16[2,352,768]{2,1,0:T(8,128)(2,1)S(1)}, bf16[2,352,768]{2,1,0:T(8,128)(2,1)S(1)}, u32[]{:S(2)}, u32[]{:S(2)}) collective-permute-start(bf16[2,352,768]{2,1,0:T(8,128)(2,1)S(1)} %add_convert_fusion.2), channel_id=1, source_target_pairs={{0,1},{1,0},{2,3},{3,2},{4,7},{5,6},{6,5},{7,4},{8,9},{9,8},{10,11... | collective-permute-start | bytes 3244040 | tf_op jit(solution)/shard_map/ppermute | solution.py:655
  148.7 8.7 %collective-permute-done.21 = bf16[4,96,768]{2,1,0:T(8,128)(2,1)S(1)} collective-permute-done((bf16[4,96,768]{2,1,0:T(8,128)(2,1)S(1)}, bf16[4,96,768]{2,1,0:T(8,128)(2,1)S(1)}, u32[]{:S(2)}, u32[]{:S(2)}) %collective-permute-start.21) | collective-permute-done | bytes 589856 | tf_op jit(solution)/shard_map/ppermute | solution.py:666
  161.5 12.9 %collective-permute-done.22 = bf16[352,768]{1,0:T(8,128)(2,1)S(1)} collective-permute-done((bf16[352,768]{1,0:T(8,128)(2,1)S(1)}, bf16[352,768]{1,0:T(8,128)(2,1)S(1)}, u32[]{:S(2)}, u32[]{:S(2)}) %collective-permute-start.22) | collective-permute-done | bytes 540704 | tf_op jit(solution)/shard_map/ppermute | solution.py:655
  179.4 6.1 %collective-permute-done.25 = bf16[224,768]{1,0:T(8,128)(2,1)S(1)} collective-permute-done((bf16[224,768]{1,0:T(8,128)(2,1)S(1)}, bf16[224,768]{1,0:T(8,128)(2,1)S(1)}, u32[]{:S(2)}, u32[]{:S(2)}) %collective-permute-start.25) | collective-permute-done | bytes 344096 | tf_op jit(solution)/shard_map/ppermute | solution.py:655
  189.1 4.9 %collective-permute-done.27 = bf16[224,768]{1,0:T(8,128)(2,1)S(1)} collective-permute-done((bf16[224,768]{1,0:T(8,128)(2,1)S(1)}, bf16[224,768]{1,0:T(8,128)(2,1)S(1)}, u32[]{:S(2)}, u32[]{:S(2)}) %collective-permute-start.27) | collective-permute-done | bytes 344096 | tf_op jit(solution)/shard_map/ppermute | solution.py:666
  195.8 5.8 %collective-permute-done.29 = bf16[224,768]{1,0:T(8,128)(2,1)S(1)} collective-permute-done((bf16[224,768]{1,0:T(8,128)(2,1)S(1)}, bf16[224,768]{1,0:T(8,128)(2,1)S(1)}, u32[]{:S(2)}, u32[]{:S(2)}) %collective-permute-start.29) | collective-permute-done | bytes 344096 | tf_op jit(solution)/shard_map/ppermute | solution.py:666
  205.6 3.9 %all-to-all-start.1 = ((bf16[4,2,64,768]{3,2,1,0:T(8,128)(2,1)}), bf16[4,2,64,768]{3,2,1,0:T(8,128)(2,1)S(1)}, u32[]{:S(2)}, u32[]{:S(2)}) async-start(bf16[4,2,64,768]{3,2,1,0:T(8,128)(2,1)} %get-tuple-element.128), calls=%async_computation.1 | async-start | bytes 1572864 | tf_op jit(solution)/shard_map/all_to_all | solution.py:685
  216.3 3.4 %collective-permute-done.32 = bf16[224,768]{1,0:T(8,128)(2,1)S(1)} collective-permute-done((bf16[224,768]{1,0:T(8,128)(2,1)S(1)}, bf16[224,768]{1,0:T(8,128)(2,1)S(1)}, u32[]{:S(2)}, u32[]{:S(2)}) %collective-permute-start.32) | collective-permute-done | bytes 344096 | tf_op jit(solution)/shard_map/ppermute | solution.py:666
  219.7 2.8 %collective-permute-done.33 = bf16[224,768]{1,0:T(8,128)(2,1)S(1)} collective-permute-done((bf16[224,768]{1,0:T(8,128)(2,1)S(1)}, bf16[224,768]{1,0:T(8,128)(2,1)S(1)}, u32[]{:S(2)}, u32[]{:S(2)}) %collective-permute-start.33) | collective-permute-done | bytes 344096 | tf_op jit(solution)/shard_map/ppermute | solution.py:666
  222.6 5.5 %collective-permute-start.34 = (bf16[1248,768]{1,0:T(8,128)(2,1)S(1)}, bf16[1248,768]{1,0:T(8,128)(2,1)S(1)}, u32[]{:S(2)}, u32[]{:S(2)}) collective-permute-start(bf16[1248,768]{1,0:T(8,128)(2,1)S(1)} %constant_dynamic-update-slice_fusion.mine), channel_id=1, source_target_pairs={{0,4},{4,0},{1,5},{5,1},{2,6},{6,2},{3,7},{7,3},{8,12},{12,8},{9,1... | collective-permute-start | bytes 5750792 | tf_op jit(solution)/shard_map/ppermute | solution.py:670
  228.1 3.5 %collective-permute-done.34.other = bf16[1248,768]{1,0:T(8,128)(2,1)S(1)} collective-permute-done((bf16[1248,768]{1,0:T(8,128)(2,1)S(1)}, bf16[1248,768]{1,0:T(8,128)(2,1)S(1)}, u32[]{:S(2)}, u32[]{:S(2)}) %collective-permute-start.34) | collective-permute-done | bytes 1916960 | tf_op jit(solution)/shard_map/ppermute | solution.py:670
  231.6 4.4 %finish.1 = (f32[192,768]{1,0:T(8,128)}, f32[192,768]{1,0:T(8,128)}, f32[192,768]{1,0:T(8,128)}, f32[128,768]{1,0:T(8,128)}, f32[768,768]{1,0:T(8,128)}, /*index...) custom-call(s32[16]{0:T(128)S(1)} %copy-done.8, ...), custom_call_target="tpu_custom_call" | custom-call | tf_op jit(solution)/shard_map/finish/pallas_call | solution.py:636
  (129 shorter events, 63.2 us)
Async XLA Ops:
  6.2 20.6 %collective-permute-start = (bf16[576,768]{1,0:T(8,128)(2,1)}, bf16[576,768]{1,0:T(8,128)(2,1)S(1)}, u32[]{:S(2)}, u32[]{:S(2)}) collective-permute-start(bf16[576,768]{1,0:T(8,128)(2,1)} %get-tuple-element.79), channel_id=1, source_target_pairs={{0,1},{1,0},{2,3},{3,2},{4,7},{5,6},{6,5},{7,4},{8,9},{9,8},{10,11... | collective-permute-start | bytes 2654216 | tf_op jit(solution)/shard_map/ppermute | solution.py:655
  8.8 26.4 %collective-permute-start.1 = (bf16[576,768]{1,0:T(8,128)(2,1)}, bf16[576,768]{1,0:T(8,128)(2,1)}, u32[]{:S(2)}, u32[]{:S(2)}) collective-permute-start(bf16[576,768]{1,0:T(8,128)(2,1)} %get-tuple-element.79), channel_id=1, source_target_pairs={{0,3},{1,2},{2,1},{3,0},{4,5},{5,4},{6,7},{7,6},{8,11},{9,10},{10,... | collective-permute-start | bytes 2654216 | tf_op jit(solution)/shard_map/ppermute | solution.py:655
  26.8 12.8 %collective-permute-start.2 = (bf16[576,768]{1,0:T(8,128)(2,1)S(1)}, bf16[576,768]{1,0:T(8,128)(2,1)}, u32[]{:S(2)}, u32[]{:S(2)}) collective-permute-start(bf16[576,768]{1,0:T(8,128)(2,1)S(1)} %collective-permute-done.p0.rest_0_), channel_id=1, source_target_pairs={{0,3},{1,2},{2,1},{3,0},{4,5},{5,4},{6,7},{7,6},{8,11},{9,10},{10,... | collective-permute-start | bytes 2654216 | tf_op jit(solution)/shard_map/ppermute | solution.py:655
  27.6 28.2 %all-to-all-start = ((bf16[4,2,64,768]{3,2,1,0:T(8,128)(2,1)}), bf16[4,2,64,768]{3,2,1,0:T(8,128)(2,1)S(1)}, u32[]{:S(2)}, u32[]{:S(2)}) async-start(bf16[4,2,64,768]{3,2,1,0:T(8,128)(2,1)} %get-tuple-element.78), calls=%async_computation | async-start | bytes 1572864 | tf_op jit(solution)/shard_map/all_to_all | solution.py:685
  32.5 23.2 %collective-permute-start.3 = (bf16[576,768]{1,0:T(8,128)(2,1)S(1)}, bf16[576,768]{1,0:T(8,128)(2,1)}, u32[]{:S(2)}, u32[]{:S(2)}) collective-permute-start(bf16[576,768]{1,0:T(8,128)(2,1)S(1)} %collective-permute-done.p0.rest_0_), channel_id=1, source_target_pairs={{0,4},{4,0},{1,5},{5,1},{2,6},{6,2},{3,7},{7,3},{8,12},{12,8},{9,1... | collective-permute-start | bytes 2654216 | tf_op jit(solution)/shard_map/ppermute | solution.py:670
  35.2 20.6 %collective-permute-start.4 = (bf16[576,768]{1,0:T(8,128)(2,1)}, bf16[576,768]{1,0:T(8,128)(2,1)}, u32[]{:S(2)}, u32[]{:S(2)}) collective-permute-start(bf16[576,768]{1,0:T(8,128)(2,1)} %collective-permute-done.1.p1.rest_1_), channel_id=1, source_target_pairs={{0,4},{4,0},{1,5},{5,1},{2,6},{6,2},{3,7},{7,3},{8,12},{12,8},{9,1... | collective-permute-start | bytes 2654216 | tf_op jit(solution)/shard_map/ppermute | solution.py:670
  39.6 16.2 %collective-permute-start.5 = (bf16[576,768]{1,0:T(8,128)(2,1)}, bf16[576,768]{1,0:T(8,128)(2,1)}, u32[]{:S(2)}, u32[]{:S(2)}) collective-permute-start(bf16[576,768]{1,0:T(8,128)(2,1)} %collective-permute-done.2.p2.rest_2_), channel_id=1, source_target_pairs={{0,4},{4,0},{1,5},{5,1},{2,6},{6,2},{3,7},{7,3},{8,12},{12,8},{9,1... | collective-permute-start | bytes 2654216 | tf_op jit(solution)/shard_map/ppermute | solution.py:670
  51.9 14.8 %collective-permute-start.6 = (bf16[3,224,768]{2,1,0:T(8,128)(2,1)}, bf16[3,224,768]{2,1,0:T(8,128)(2,1)}, u32[]{:S(2)}, u32[]{:S(2)}) collective-permute-start(bf16[3,224,768]{2,1,0:T(8,128)(2,1)} %pad_maximum_fusion), channel_id=1, source_target_pairs={{0,32},{4,12},{8,40},{12,4},{16,48},{20,28},{24,56},{28,20},{32,0}... | collective-permute-start | bytes 3096584 | tf_op jit(solution)/shard_map/ppermute | solution.py:666
  53.5 15.0 %collective-permute-start.7 = (bf16[3,224,768]{2,1,0:T(8,128)(2,1)}, bf16[3,224,768]{2,1,0:T(8,128)(2,1)}, u32[]{:S(2)}, u32[]{:S(2)}) collective-permute-start(bf16[3,224,768]{2,1,0:T(8,128)(2,1)} %pad_maximum_fusion), channel_id=1, source_target_pairs={{0,96},{4,28},{8,104},{12,20},{16,112},{20,12},{24,120},{28,4},{32... | collective-permute-start | bytes 3096584 | tf_op jit(solution)/shard_map/ppermute | solution.py:666
  68.5 12.8 %collective-permute-start.8 = (bf16[3,224,768]{2,1,0:T(8,128)(2,1)}, bf16[3,224,768]{2,1,0:T(8,128)(2,1)S(1)}, u32[]{:S(2)}, u32[]{:S(2)}) collective-permute-start(bf16[3,224,768]{2,1,0:T(8,128)(2,1)} %collective-permute-done.6.rest_3_), channel_id=1, source_target_pairs={{0,4},{4,0},{1,5},{5,1},{2,6},{6,2},{3,7},{7,3},{8,12},{12,8},{9,1... | collective-permute-start | bytes 3096584 | tf_op jit(solution)/shard_map/ppermute | solution.py:670
  68.5 12.8 %collective-permute-start.9 = (bf16[3,224,768]{2,1,0:T(8,128)(2,1)}, bf16[3,224,768]{2,1,0:T(8,128)(2,1)S(1)}, u32[]{:S(2)}, u32[]{:S(2)}) collective-permute-start(bf16[3,224,768]{2,1,0:T(8,128)(2,1)} %collective-permute-done.7.rest_4_), channel_id=1, source_target_pairs={{0,4},{4,0},{1,5},{5,1},{2,6},{6,2},{3,7},{7,3},{8,12},{12,8},{9,1... | collective-permute-start | bytes 3096584 | tf_op jit(solution)/shard_map/ppermute | solution.py:670
  71.2 10.2 %collective-permute-start.10 = (bf16[3,128,768]{2,1,0:T(8,128)(2,1)S(1)}, bf16[3,128,768]{2,1,0:T(8,128)(2,1)S(1)}, u32[]{:S(2)}, u32[]{:S(2)}) collective-permute-start(bf16[3,128,768]{2,1,0:T(8,128)(2,1)S(1)} %slice.132), channel_id=1, source_target_pairs={{0,96},{4,28},{8,104},{12,20},{16,112},{20,12},{24,120},{28,4},{32... | collective-permute-start | bytes 1769480 | tf_op jit(solution)/shard_map/ppermute | solution.py:666
  107.5 9.1 %collective-permute-start.15 = (bf16[4,4,96,768]{3,2,1,0:T(8,128)(2,1)}, bf16[4,4,96,768]{3,2,1,0:T(8,128)(2,1)S(1)}, u32[]{:S(2)}, u32[]{:S(2)}) collective-permute-start(bf16[4,4,96,768]{3,2,1,0:T(8,128)(2,1)} %get-tuple-element.105), channel_id=1, source_target_pairs={{0,4},{4,0},{1,5},{5,1},{2,6},{6,2},{3,7},{7,3},{8,12},{12,8},{9,1... | collective-permute-start | bytes 7077896 | tf_op jit(solution)/shard_map/ppermute | solution.py:670
  114.2 21.6 %collective-permute-start.16 = (bf16[2,4,128,768]{3,2,1,0:T(8,128)(2,1)S(1)}, bf16[2,4,128,768]{3,2,1,0:T(8,128)(2,1)S(1)}, u32[]{:S(2)}, u32[]{:S(2)}) collective-permute-start(bf16[2,4,128,768]{3,2,1,0:T(8,128)(2,1)S(1)} %add_convert_fusion), channel_id=1, source_target_pairs={{0,32},{4,12},{8,40},{12,4},{16,48},{20,28},{24,56},{28,20},{32,0}... | collective-permute-start | bytes 4718600 | tf_op jit(solution)/shard_map/ppermute | solution.py:666
  118.0 17.8 %collective-permute-start.17 = (bf16[2,4,96,768]{3,2,1,0:T(8,128)(2,1)S(1)}, bf16[2,4,96,768]{3,2,1,0:T(8,128)(2,1)}, u32[]{:S(2)}, u32[]{:S(2)}) collective-permute-start(bf16[2,4,96,768]{3,2,1,0:T(8,128)(2,1)S(1)} %add_convert_fusion.1), channel_id=1, source_target_pairs={{0,96},{4,28},{8,104},{12,20},{16,112},{20,12},{24,120},{28,4},{32... | collective-permute-start | bytes 3538952 | tf_op jit(solution)/shard_map/ppermute | solution.py:666
  140.6 16.8 %collective-permute-start.19 = (bf16[2,352,768]{2,1,0:T(8,128)(2,1)S(1)}, bf16[2,352,768]{2,1,0:T(8,128)(2,1)S(1)}, u32[]{:S(2)}, u32[]{:S(2)}) collective-permute-start(bf16[2,352,768]{2,1,0:T(8,128)(2,1)S(1)} %add_convert_fusion.2), channel_id=1, source_target_pairs={{0,1},{1,0},{2,3},{3,2},{4,7},{5,6},{6,5},{7,4},{8,9},{9,8},{10,11... | collective-permute-start | bytes 3244040 | tf_op jit(solution)/shard_map/ppermute | solution.py:655
  144.5 12.9 %collective-permute-start.20 = (bf16[4,128,768]{2,1,0:T(8,128)(2,1)S(1)}, bf16[4,128,768]{2,1,0:T(8,128)(2,1)S(1)}, u32[]{:S(2)}, u32[]{:S(2)}) collective-permute-start(bf16[4,128,768]{2,1,0:T(8,128)(2,1)S(1)} %fusion.3), channel_id=1, source_target_pairs={{0,96},{4,28},{8,104},{12,20},{16,112},{20,12},{24,120},{28,4},{32... | collective-permute-start | bytes 2359304 | tf_op jit(solution)/shard_map/ppermute | solution.py:666
  159.4 16.9 %collective-permute-start.23 = (bf16[2,224,768]{2,1,0:T(8,128)(2,1)S(1)}, bf16[2,224,768]{2,1,0:T(8,128)(2,1)S(1)}, u32[]{:S(2)}, u32[]{:S(2)}) collective-permute-start(bf16[2,224,768]{2,1,0:T(8,128)(2,1)S(1)} %fusion.4), channel_id=1, source_target_pairs={{0,1},{1,0},{2,3},{3,2},{4,7},{5,6},{6,5},{7,4},{8,9},{9,8},{10,11... | collective-permute-start | bytes 2064392 | tf_op jit(solution)/shard_map/ppermute | solution.py:655
  161.5 12.9 %collective-permute-start.22 = (bf16[352,768]{1,0:T(8,128)(2,1)S(1)}, bf16[352,768]{1,0:T(8,128)(2,1)S(1)}, u32[]{:S(2)}, u32[]{:S(2)}) collective-permute-start(bf16[352,768]{1,0:T(8,128)(2,1)S(1)} %fusion.7), channel_id=1, source_target_pairs={{0,3},{1,2},{2,1},{3,0},{4,5},{5,4},{6,7},{7,6},{8,11},{9,10},{10,... | collective-permute-start | bytes 1622024 | tf_op jit(solution)/shard_map/ppermute | solution.py:655
  176.6 9.4 %collective-permute-start.24 = (bf16[352,768]{1,0:T(8,128)(2,1)S(1)}, bf16[352,768]{1,0:T(8,128)(2,1)S(1)}, u32[]{:S(2)}, u32[]{:S(2)}) collective-permute-start(bf16[352,768]{1,0:T(8,128)(2,1)S(1)} %fusion.2), channel_id=1, source_target_pairs={{0,8},{4,36},{8,0},{12,44},{16,24},{20,52},{24,16},{28,60},{32,40}... | collective-permute-start | bytes 1622024 | tf_op jit(solution)/shard_map/ppermute | solution.py:666
  203.5 10.1 %collective-permute-start.30 = (bf16[352,768]{1,0:T(8,128)(2,1)S(1)}, bf16[352,768]{1,0:T(8,128)(2,1)}, u32[]{:S(2)}, u32[]{:S(2)}) collective-permute-start(bf16[352,768]{1,0:T(8,128)(2,1)S(1)} %add_convert_fusion.6), channel_id=1, source_target_pairs={{0,96},{4,28},{8,104},{12,20},{16,112},{20,12},{24,120},{28,4},{32... | collective-permute-start | bytes 1622024 | tf_op jit(solution)/shard_map/ppermute | solution.py:666
  205.6 16.9 %all-to-all-start.1 = ((bf16[4,2,64,768]{3,2,1,0:T(8,128)(2,1)}), bf16[4,2,64,768]{3,2,1,0:T(8,128)(2,1)S(1)}, u32[]{:S(2)}, u32[]{:S(2)}) async-start(bf16[4,2,64,768]{3,2,1,0:T(8,128)(2,1)} %get-tuple-element.128), calls=%async_computation.1 | async-start | bytes 1572864 | tf_op jit(solution)/shard_map/all_to_all | solution.py:685
  209.7 9.9 %collective-permute-start.32 = (bf16[224,768]{1,0:T(8,128)(2,1)S(1)}, bf16[224,768]{1,0:T(8,128)(2,1)S(1)}, u32[]{:S(2)}, u32[]{:S(2)}) collective-permute-start(bf16[224,768]{1,0:T(8,128)(2,1)S(1)} %add_convert_fusion.10), channel_id=1, source_target_pairs={{0,64},{4,20},{8,72},{12,28},{16,80},{20,4},{24,88},{28,12},{32,96... | collective-permute-start | bytes 1032200 | tf_op jit(solution)/shard_map/ppermute | solution.py:666
  211.2 11.3 %collective-permute-start.33 = (bf16[224,768]{1,0:T(8,128)(2,1)S(1)}, bf16[224,768]{1,0:T(8,128)(2,1)S(1)}, u32[]{:S(2)}, u32[]{:S(2)}) collective-permute-start(bf16[224,768]{1,0:T(8,128)(2,1)S(1)} %add_convert_fusion.10), channel_id=1, source_target_pairs={{0,96},{4,28},{8,104},{12,20},{16,112},{20,12},{24,120},{28,4},{32... | collective-permute-start | bytes 1032200 | tf_op jit(solution)/shard_map/ppermute | solution.py:666
  (30 other events, 224.6 us)
